TPU v7x, 512 devices: a whole 4x4x16 slice. The times are simulated.
512 devices in a mesh: gx: 128 (over x_lo, z, y), gy: 4 (over x_hi, core).
Axes of the slice: x: 4 (x_hi: 2, x_lo: 2; x = x_hi * 2 + x_lo), y: 4, z: 16, core: 2. Of those that a mesh axis runs over, the one named last changes fastest.
Arguments:
- populations: float32 [19, 1024, 64, 128], P(None, 'gx', 'gy'), as said below
- order_field: float32 [1024, 64, 128], P('gx', 'gy'), may hold values from -1 to 1
- solid_flags: int32 [1024, 64, 128], P('gx', 'gy'), may hold values 0 or 1
- plane_flags: int32 [128], replicated, may hold values 0 or 1
- shear_shift: int32 [1], replicated, may hold values from 1 to 63
- link_site: int32 [524288], P(('gx', 'gy')), may hold values from 0 to 16383, as said below
- link_dir: int32 [524288], P(('gx', 'gy')), may hold values from 1 to 18
- link_colloid: int32 [524288], P(('gx', 'gy')), may hold values from 0 to 2047
- link_count: int32 [4096], P(('gx', 'gy')), may hold values from 1 to 128, 327680 in all
- colloid_slot: int32 [2048], replicated, may hold values from 0 to 2047, each once
- colloid_speed: float32 [3, 2048], replicated, may hold values from -0.6 to 0.6
Outputs:
- new_populations: float32 [19, 1024, 64, 128], P(None, 'gx', 'gy')
- new_order: float32 [1024, 64, 128], P('gx', 'gy')
- colloid_force: float32 [3, 2048], P(None, ('gx', 'gy'))
Inputs may be any that keep to these rules, and one draw needn't show every extreme that they name: `populations`: populations lie between 0.2 w_i and 1.8 w_i. `link_site`: the slots of one device name distinct sites in rising order, one in each run of (8 * 16 * 128) / 1024 sites.
All inputs are finite; a program needn't handle non-finite values. No bound on the sum of `solid_flags` or of `link_count` on one device may be relied on, other than what follows from the above.
Results may differ from a plain program's by a relative error of at most 0.00002.
Values sent between devices are 32-bit elements; how exact they have to be, the bound alone decides.
A program may use at most 64 MiB of HBM per device.

v0:
```python
import jax
import jax.numpy as jnp
from jax import lax
from jax.sharding import PartitionSpec as P

VELOCITIES = [
    [0, 0, 0],
    [1, 0, 0],
    [-1, 0, 0],
    [0, 1, 0],
    [0, -1, 0],
    [0, 0, 1],
    [0, 0, -1],
    [1, 1, 0],
    [-1, -1, 0],
    [1, -1, 0],
    [-1, 1, 0],
    [1, 0, 1],
    [-1, 0, -1],
    [1, 0, -1],
    [-1, 0, 1],
    [0, 1, 1],
    [0, -1, -1],
    [0, 1, -1],
    [0, -1, 1],
]
WEIGHTS = [1.0 / 3.0] + [1.0 / 18.0] * 6 + [1.0 / 36.0] * 12
OPPOSITE = [0, 2, 1, 4, 3, 6, 5, 8, 7, 10, 9, 12, 11, 14, 13, 16, 15, 18, 17]
UP_X = [1, 7, 9, 11, 13]
DOWN_X = [2, 8, 10, 12, 14]
UP_Y = [3, 7, 10, 15, 17]
DOWN_Y = [4, 8, 9, 16, 18]
TAU = 0.8
BULK = 0.04
KAPPA = 0.04
MOBILITY = 0.2
PLANE_SPEED = 0.05


def padded_2(block, sides, width):
    for axis, dim in sides:
        count = lax.axis_size(axis)
        forward = [(i, i + 1) for i in range(count - 1)]
        forward.append((count - 1, 0))
        backward = [(target, source) for source, target in forward]
        low = lax.ppermute(
            lax.slice_in_dim(block, block.shape[dim] - width, None, axis=dim), axis, forward
        )
        high = lax.ppermute(lax.slice_in_dim(block, 0, width, axis=dim), axis, backward)
        block = jnp.concatenate([low, block, high], axis=dim)
    return block


def moments(stack):
    velocity_table = jnp.array(VELOCITIES, jnp.float32)
    shape = (19,) + (1,) * (stack.ndim - 1)
    density = jnp.sum(stack, axis=0)
    speed_x = jnp.sum(stack * velocity_table[:, 0].reshape(shape), axis=0) / density
    speed_y = jnp.sum(stack * velocity_table[:, 1].reshape(shape), axis=0) / density
    speed_z = jnp.sum(stack * velocity_table[:, 2].reshape(shape), axis=0) / density
    return (density, speed_x, speed_y, speed_z)


def boost_face(face, components, change):
    density, speed_x, speed_y, speed_z = moments(face)
    result = []
    for component in components:
        east_step, north_step, upward_step = VELOCITIES[component]
        weight = WEIGHTS[component]
        projection = east_step * speed_x + north_step * speed_y + upward_step * speed_z
        shifted = projection + north_step * change
        square_old = speed_x * speed_x + speed_y * speed_y + speed_z * speed_z
        moved_y = speed_y + change
        square_new = speed_x * speed_x + moved_y * moved_y + speed_z * speed_z
        correction = (
            weight
            * density
            * (
                3.0 * (shifted - projection)
                + 4.5 * (shifted * shifted - projection * projection)
                - 1.5 * (square_new - square_old)
            )
        )
        result.append(face[component] + correction)
    return jnp.stack(result)


def collide(read, force_x, force_y, force_z):
    velocity_table = jnp.array(VELOCITIES, jnp.float32)
    shape = (19,) + (1,) * (read.ndim - 1)
    density = jnp.sum(read, axis=0)
    speed_x = (
        jnp.sum(read * velocity_table[:, 0].reshape(shape), axis=0) + 0.5 * force_x
    ) / density
    speed_y = (
        jnp.sum(read * velocity_table[:, 1].reshape(shape), axis=0) + 0.5 * force_y
    ) / density
    speed_z = (
        jnp.sum(read * velocity_table[:, 2].reshape(shape), axis=0) + 0.5 * force_z
    ) / density
    square = speed_x * speed_x + speed_y * speed_y + speed_z * speed_z
    outputs = []
    for component in range(19):
        east_step, north_step, upward_step = VELOCITIES[component]
        weight = WEIGHTS[component]
        projection = east_step * speed_x + north_step * speed_y + upward_step * speed_z
        balance = (
            weight
            * density
            * (1.0 + 3.0 * projection + 4.5 * projection * projection - 1.5 * square)
        )
        along_force = east_step * force_x + north_step * force_y + upward_step * force_z
        forcing = weight * (
            3.0
            * (
                (east_step - speed_x) * force_x
                + (north_step - speed_y) * force_y
                + (upward_step - speed_z) * force_z
            )
            + 9.0 * projection * along_force
        )
        outputs.append(
            read[component] - (read[component] - balance) / TAU + (1.0 - 0.5 / TAU) * forcing
        )
    return (jnp.stack(outputs), speed_x, speed_y, speed_z)


def laplace(values):
    center = values[1:-1, 1:-1]
    return (
        values[2:, 1:-1]
        + values[:-2, 1:-1]
        + values[1:-1, 2:]
        + values[1:-1, :-2]
        + jnp.roll(center, -1, 2)
        + jnp.roll(center, 1, 2)
        - 6.0 * center
    )


def gradient(values):
    center = values[1:-1, 1:-1]
    return (
        (values[2:, 1:-1] - values[:-2, 1:-1]) * 0.5,
        (values[1:-1, 2:] - values[1:-1, :-2]) * 0.5,
        (jnp.roll(center, -1, 2) - jnp.roll(center, 1, 2)) * 0.5,
    )


def per_device(
    populations,
    order_field,
    solid_flags,
    plane_flags,
    shear_shift,
    link_site,
    link_dir,
    link_colloid,
    link_count,
    colloid_slot,
    colloid_speed,
):
    slab_index = lax.axis_index("gx")
    slab_count = lax.axis_size("gx")
    pencil_index = lax.axis_index("gy")
    pencil_count = lax.axis_size("gy")
    slab_depth, pencil_width, column_height = order_field.shape
    total_rows = pencil_width * pencil_count
    plane_shift = shear_shift[0]
    plane_low = plane_flags[slab_index]
    plane_high = plane_flags[(slab_index + 1) % slab_count]
    low_offset = plane_shift * plane_low
    high_offset = plane_shift * plane_high
    low_face = populations[:, 0]
    high_face = populations[:, slab_depth - 1]
    down_plain = jnp.stack([low_face[component] for component in DOWN_X])
    up_plain = jnp.stack([high_face[component] for component in UP_X])
    down_going = jnp.where(plane_low == 1, boost_face(low_face, DOWN_X, PLANE_SPEED), down_plain)
    up_going = jnp.where(plane_high == 1, boost_face(high_face, UP_X, -PLANE_SPEED), up_plain)
    low_message = jnp.concatenate([down_going, order_field[0:2]], axis=0)
    high_message = jnp.concatenate([up_going, order_field[slab_depth - 2 : slab_depth]], axis=0)

    def window(gathered, first_row):
        doubled = jnp.concatenate([gathered, gathered], axis=1)
        begin = jnp.mod(first_row, total_rows)
        return lax.dynamic_slice_in_dim(doubled, begin, pencil_width + 4, 1)

    packed = jnp.stack([low_message, high_message], axis=1)
    arrived = padded_2(packed, (("gx", 1),), 1)
    incoming = jnp.stack([arrived[:, 0], arrived[:, 3]], axis=0)
    gathered = lax.all_gather(incoming, "gy", axis=2, tiled=True)
    below = window(gathered[0], pencil_index * pencil_width - 2 - low_offset)
    above = window(gathered[1], pencil_index * pencil_width - 2 + high_offset)
    low_rows = jnp.concatenate(
        [
            jnp.stack([populations[component, :, 0] for component in DOWN_Y]),
            order_field[None, :, 0],
            order_field[None, :, 1],
        ],
        axis=0,
    )
    high_rows = jnp.concatenate(
        [
            jnp.stack([populations[component, :, pencil_width - 1] for component in UP_Y]),
            order_field[None, :, pencil_width - 2],
            order_field[None, :, pencil_width - 1],
        ],
        axis=0,
    )
    rims = padded_2(jnp.stack([low_rows, high_rows], axis=2), (("gy", 2),), 1)
    from_below = rims[:, :, 0]
    from_above = rims[:, :, 3]
    middle = jnp.concatenate(
        [
            from_below[5][:, None],
            from_below[6][:, None],
            order_field,
            from_above[5][:, None],
            from_above[6][:, None],
        ],
        axis=1,
    )
    padded = jnp.concatenate(
        [below[5][None], below[6][None], middle, above[5][None], above[6][None]], axis=0
    )
    inner_order = padded[1:-1, 1:-1]
    potential = BULK * (inner_order * inner_order * inner_order - inner_order) - KAPPA * laplace(
        padded
    )
    slope_x, slope_y, slope_z = gradient(potential)
    phase_x, phase_y, phase_z = gradient(inner_order)
    potential_curve = laplace(potential)
    zero_row = jnp.zeros((slab_depth, 1, column_height), jnp.float32)
    zero_layer = jnp.zeros((1, pencil_width + 2, column_height), jnp.float32)
    pieces = []
    for component in range(19):
        east_step, north_step, upward_step = VELOCITIES[component]
        low_row = from_below[UP_Y.index(component)][:, None] if north_step == 1 else zero_row
        high_row = from_above[DOWN_Y.index(component)][:, None] if north_step == -1 else zero_row
        extended = jnp.concatenate([low_row, populations[component], high_row], axis=1)
        left_layer = (
            below[UP_X.index(component), 1 : pencil_width + 3][None]
            if east_step == 1
            else zero_layer
        )
        right_layer = (
            above[DOWN_X.index(component), 1 : pencil_width + 3][None]
            if east_step == -1
            else zero_layer
        )
        extended = jnp.concatenate([left_layer, extended, right_layer], axis=0)
        pulled = extended[
            1 - east_step : 1 - east_step + slab_depth,
            1 - north_step : 1 - north_step + pencil_width,
        ]
        pieces.append(jnp.roll(pulled, upward_step, 2))
    read = jnp.stack(pieces)
    velocity_table = jnp.array(VELOCITIES, jnp.float32)
    weight_table = jnp.array(WEIGHTS, jnp.float32)
    opposite_table = jnp.array(OPPOSITE, jnp.int32)
    flat_stream = read.reshape((19, -1))
    flat_post = populations.reshape((19, -1))
    position = jnp.arange(link_site.shape[0], dtype=jnp.int32)
    live_links = position % 128 < link_count[position // 128]
    source = flat_post[link_dir, link_site]
    direction_vec = velocity_table[link_dir]
    link_weight = weight_table[link_dir]
    link_speed = colloid_speed[:, link_colloid]
    projection = jnp.sum(direction_vec.T * link_speed, axis=0)
    returned = source - 6.0 * link_weight * projection
    target = opposite_table[link_dir]
    current = flat_stream[target, link_site]
    flat_stream = flat_stream.at[target, link_site].set(jnp.where(live_links, returned, current))
    read = flat_stream.reshape(read.shape)
    transfer = (
        jnp.where(live_links, 2.0 * source - 6.0 * link_weight * projection, 0.0) * direction_vec.T
    )
    partial_value = jax.ops.segment_sum(
        transfer.T, colloid_slot[link_colloid], num_segments=colloid_slot.shape[0]
    ).T
    colloid_force = lax.psum_scatter(partial_value, ("gx", "gy"), scatter_dimension=1, tiled=True)
    collided, speed_x, speed_y, speed_z = collide(
        read, -order_field * slope_x, -order_field * slope_y, -order_field * slope_z
    )
    solid_mask = solid_flags == 1
    weight_shape = weight_table.reshape((19, 1, 1, 1))
    new_populations = jnp.where(solid_mask[None], weight_shape + 0.0 * collided, collided)
    advanced = (
        order_field
        - (speed_x * phase_x + speed_y * phase_y + speed_z * phase_z)
        + MOBILITY * potential_curve
    )
    new_order = jnp.where(solid_mask, order_field, advanced)
    return (new_populations, new_order, colloid_force)


def solution(mesh):
    return jax.shard_map(
        per_device,
        mesh=mesh,
        in_specs=(
            P(None, "gx", "gy", None),
            P("gx", "gy", None),
            P("gx", "gy", None),
            P(),
            P(),
            P(("gx", "gy")),
            P(("gx", "gy")),
            P(("gx", "gy")),
            P(("gx", "gy")),
            P(),
            P(),
        ),
        out_specs=(P(None, "gx", "gy", None), P("gx", "gy", None), P(None, ("gx", "gy"))),
        check_vma=False,
    )
```

profile of v0, /device:TPU:1, one launch (start us, length us, event | category | flops | bytes accessed | tf_op | source)
XLA Modules:
  0.0 232.4 jit_solution(17619595374594204179)
XLA Ops:
  0.7 1.0 bitcast_reduce_fusion
  1.7 0.9 slice_reduce_fusion
  2.7 0.7 fusion.273
  3.4 1.4 fusion.277
  5.4 1.1 fusion.4
  6.6 0.7 constant_dynamic-update-slice_fusion.9
  7.3 0.7 constant_dynamic-update-slice_fusion.8
  8.1 0.7 constant_dynamic-update-slice_fusion.7
  8.8 0.7 constant_dynamic-update-slice_fusion.6
  9.6 0.6 maximum_bitcast_fusion
  10.3 4.0 %collective-permute-start = (f32[7,1,16,128]{3,2,0,1:T(8,128)}, f32[7,1,16,128]{3,2,0,1:T(8,128)S(1)}, u32[]{:S(2)}, u32[]{:S(2)}) collective-permute-start(f32[7,1,16,128]{3,2,0,1:T(8,128)} %maximum_bitcast_fusion), channel_id=1, source_target_pairs={{0,4},{4,8},{8,12},{12,16},{16,20},{20,24},{24,28},{28,32},{32,36}... | collective-permute-start | bytes 172040 | tf_op jit(solution)/shard_map/ppermute | solution.py:46
  15.0 0.6 maximum_bitcast_fusion.1
  15.7 13.2 %collective-permute-start.1 = (f32[7,1,16,128]{3,2,0,1:T(8,128)}, f32[7,1,16,128]{3,2,0,1:T(8,128)}, u32[]{:S(2)}, u32[]{:S(2)}) collective-permute-start(f32[7,1,16,128]{3,2,0,1:T(8,128)} %maximum_bitcast_fusion.1), channel_id=1, source_target_pairs={{4,0},{8,4},{12,8},{16,12},{20,16},{24,20},{28,24},{32,28},{36,32}... | collective-permute-start | bytes 172040 | tf_op jit(solution)/shard_map/ppermute | solution.py:49
  29.0 0.6 constant_dynamic-update-slice_fusion.26
  29.5 0.6 constant_dynamic-update-slice_fusion.25
  30.1 0.6 constant_dynamic-update-slice_fusion.24
  30.7 0.6 constant_dynamic-update-slice_fusion.23
  31.3 0.6 constant_dynamic-update-slice_fusion.22
  31.9 0.6 constant_dynamic-update-slice_fusion.21
  32.5 0.6 constant_dynamic-update-slice_fusion.20
  33.1 5.2 %collective-permute-start.2 = (f32[7,8,1,128]{3,1,2,0:T(8,128)}, f32[7,8,1,128]{3,1,2,0:T(8,128)}, u32[]{:S(2)}, u32[]{:S(2)}) collective-permute-start(f32[7,8,1,128]{3,1,2,0:T(8,128)} %bitcast.45), channel_id=1, source_target_pairs={{0,1},{1,2},{2,3},{3,0},{4,5},{5,6},{6,7},{7,4},{8,9},{9,10},{10,1... | collective-permute-start | bytes 86024 | tf_op jit(solution)/shard_map/ppermute | solution.py:46
  38.3 0.6 constant_dynamic-update-slice_fusion.33
  38.9 0.6 constant_dynamic-update-slice_fusion.32
  39.5 0.6 constant_dynamic-update-slice_fusion.31
  40.1 0.6 constant_dynamic-update-slice_fusion.30
  40.7 0.6 constant_dynamic-update-slice_fusion.29
  41.3 0.6 constant_dynamic-update-slice_fusion.28
  41.8 0.6 constant_dynamic-update-slice_fusion.27
  42.4 1.9 collective-permute-start.3
  44.4 0.8 slice_bitcast_fusion.2
  45.2 0.7 fusion.270
  45.9 0.7 fusion.271
  46.6 0.7 fusion.276
  47.5 0.9 copy.154
  48.9 8.6 %gather_fusion = f32[1024]{0:T(1024)S(1)} fusion(f32[19,16384]{1,0:T(8,128)S(1)} %bitcast.664, s32[1024]{0:T(1024)S(1)} %bitcast.582), kind=kCustom, calls=%fused_computation | custom fusion | bytes 16384 | tf_op jit(solution)/shard_map/gather | solution.py:265
  57.5 2.8 %gather_fusion.2 = f32[1024,3]{1,0:T(8,128)S(1)} fusion(f32[3,2048]{0,1:T(8,128)S(1)} %copy.134, s32[1024]{0:T(1024)S(1)} %get-tuple-element.192), kind=kCustom, calls=%fused_computation.2 | custom fusion | bytes 28672 | tf_op jit(solution)/shard_map/gather | solution.py:268
  60.3 2.8 %gather_fusion.1 = f32[1024,3]{1,0:T(8,128)S(1)} fusion(f32[19,3]{1,0:T(8,128)S(1)} %copy-done.1, s32[1024]{0:T(1024)S(1)} %get-tuple-element.162), kind=kCustom, calls=%fused_computation.1 | custom fusion | bytes 28672 | tf_op jit(solution)/shard_map/gather | solution.py:266
  63.4 4.3 %compare_select_fusion.2 = s32[1024,1]{0,1:T(1,128)S(1)} fusion(s32[]{:T(128)} %bitcast.109, s32[]{:T(128)} %bitcast.110, s32[]{:T(128)} %bitcast.111, s32[]{:T(128)} %bitcast.112, s32[]{:T(128)} %bitcast.113, s32[]{:T(128)} %bitcast.115, s32[]{:T(128)} %bitcast.114), kind=kLoop, calls=%fused_computation.412 | loop fusion | flops 23552 | bytes 4124 | tf_op jit(solution)/shard_map/gather | solution.py:264
  67.7 1.2 subtract_select_fusion
  68.9 0.7 slice.868
  69.6 0.7 slice.870
  70.5 6.2 %gather_fusion.4 = s32[1024]{0:T(1024)S(1)} fusion(s32[2048]{0:T(1024)S(1)} %copy-done, s32[1024]{0:T(1024)S(1)} %get-tuple-element.192), kind=kCustom, calls=%fused_computation.4 | custom fusion | bytes 12288 | tf_op jit(solution)/shard_map/gather | solution.py:279
  76.7 6.8 %scatter_custom_fusion = f32[2048,3]{1,0:T(8,128)S(1)} fusion(s32[1024]{0:T(1024)S(1)} %gather_fusion.4, f32[1024,3]{1,0:T(8,128)S(1)} %gather_fusion.1, f32[]{:T(128)} %constant.148.clone.1, f32[1024]{0:T(1024)S(1)} %get-tuple-element.26), kind=kCustom, calls=%fused_computation.12 | custom fusion | flops 6144 | bytes 552964 | tf_op jit(solution)/shard_map/scatter-add | solution.py:278
  83.5 104.1 %all-reduce = f32[3,2048]{0,1:T(8,128)S(1)} all-reduce(f32[3,2048]{0,1:T(8,128)S(1)} %bitcast.667), channel_id=2, replica_groups=mesh['gx'=128,'gy'=4] {'gx','gy'}, use_global_device_ids=true, to_apply=%region_15.16.clone | all-reduce | flops 6144 | bytes 49152
  187.8 0.6 broadcast_select_fusion.2
  190.4 0.7 copy.138
  191.1 0.7 fusion.275
  191.8 0.7 fusion.274
  192.7 0.7 fusion.192
  193.5 0.7 fusion.191
  194.2 0.7 fusion.194
  195.2 0.7 pad_maximum_fusion.30
  195.8 0.7 fusion.193
  196.6 0.8 pad_maximum_fusion.9
  197.4 8.5 %all_gather.3 = f32[2,7,64,128]{3,2,1,0:T(8,128)S(1)} all-gather(f32[2,7,16,128]{3,2,1,0:T(8,128)S(1)} %pad_maximum_fusion.9), channel_id=1, replica_groups=mesh['gx'=128,'gy'=4] {'gy'}, dimensions={2}, use_global_device_ids=true | all-gather | bytes 573440 | tf_op jit(solution)/shard_map/all_gather | solution.py:191
  206.4 0.7 fusion.266
  207.2 0.7 fusion.267
  209.1 2.7 %stack.185 = f32[19,16384]{1,0:T(8,128)S(1)} concatenate(f32[1,16384]{1,0:T(1,128)S(1)} %bitcast.670, f32[1,16384]{1,0:T(1,128)S(1)} %bitcast.707, f32[1,16384]{1,0:T(1,128)S(1)} %bitcast.703, f32[1,16384]{1,0:T(1,128)} %bitcast.705, f32[1,16384]{1,0:T(1,128)} %bitcast.704, f32[1,16384]{1,0:T(1,128)S(1)} %bitcast.671, f32[1,16384]{1,0:T(1,128)S(1)} %bitcast.672, ...), dimensions={0} | concatenate | bytes 2490368 | tf_op jit(solution)/shard_map/stack | solution.py:257
  212.1 8.6 %gather_fusion.3 = f32[1024]{0:T(1024)S(1)} fusion(f32[19,16384]{1,0:T(8,128)S(1)} %stack.185, s32[1024]{0:T(1024)S(1)} %bitcast.583), kind=kCustom, calls=%fused_computation.3 | custom fusion | bytes 16384 | tf_op jit(solution)/shard_map/gather | solution.py:272
  220.7 5.0 %scatter_fusion = f32[311296]{0:T(1024)S(1)} fusion(f32[311296]{0:T(1024)S(1)} %reshape.949, s32[1024]{0:T(1024)S(1)} %copy-done.33, f32[1024]{0:T(1024)S(1)} %subtract_select_fusion.1), kind=kCustom, calls=%fused_computation.6 | custom fusion | bytes 16384
  226.1 0.5 copy-done.39
  226.7 1.0 multiply_reduce_fusion.1
  227.8 0.8 fusion.181
  231.1 1.2 add_select_fusion
  (168 shorter events, 6.3 us)
Async XLA Ops:
  0.6 69.9 %copy-start = (s32[2048]{0:T(1024)S(1)}, s32[2048]{0:T(1024)}, u32[]{:S(2)}) copy-start(s32[2048]{0:T(1024)} %param.26) | copy-start | bytes 24580
  0.6 8.9 %copy-start.2 = (f32[19,8,16,128]{3,2,1,0:T(8,128)S(1)}, f32[19,8,16,128]{3,2,1,0:T(8,128)}, u32[]{:S(2)}) copy-start(f32[19,8,16,128]{3,2,1,0:T(8,128)} %param.17) | copy-start | bytes 3735556
  0.7 28.3 %copy-start.3 = (f32[8,16,128]{2,1,0:T(8,128)S(1)}, f32[8,16,128]{2,1,0:T(8,128)}, u32[]{:S(2)}) copy-start(f32[8,16,128]{2,1,0:T(8,128)} %param.18) | copy-start | bytes 196612
  10.3 186.3 %collective-permute-start = (f32[7,1,16,128]{3,2,0,1:T(8,128)}, f32[7,1,16,128]{3,2,0,1:T(8,128)S(1)}, u32[]{:S(2)}, u32[]{:S(2)}) collective-permute-start(f32[7,1,16,128]{3,2,0,1:T(8,128)} %maximum_bitcast_fusion), channel_id=1, source_target_pairs={{0,4},{4,8},{8,12},{12,16},{16,20},{20,24},{24,28},{28,32},{32,36}... | collective-permute-start | bytes 172040 | tf_op jit(solution)/shard_map/ppermute | solution.py:46
  15.7 180.9 %collective-permute-start.1 = (f32[7,1,16,128]{3,2,0,1:T(8,128)}, f32[7,1,16,128]{3,2,0,1:T(8,128)}, u32[]{:S(2)}, u32[]{:S(2)}) collective-permute-start(f32[7,1,16,128]{3,2,0,1:T(8,128)} %maximum_bitcast_fusion.1), channel_id=1, source_target_pairs={{4,0},{8,4},{12,8},{16,12},{20,16},{24,20},{28,24},{32,28},{36,32}... | collective-permute-start | bytes 172040 | tf_op jit(solution)/shard_map/ppermute | solution.py:49
  33.1 158.0 %collective-permute-start.2 = (f32[7,8,1,128]{3,1,2,0:T(8,128)}, f32[7,8,1,128]{3,1,2,0:T(8,128)}, u32[]{:S(2)}, u32[]{:S(2)}) collective-permute-start(f32[7,8,1,128]{3,1,2,0:T(8,128)} %bitcast.45), channel_id=1, source_target_pairs={{0,1},{1,2},{2,3},{3,0},{4,5},{5,6},{6,7},{7,4},{8,9},{9,10},{10,1... | collective-permute-start | bytes 86024 | tf_op jit(solution)/shard_map/ppermute | solution.py:46
  42.4 149.4 %collective-permute-start.3 = (f32[7,8,1,128]{3,1,2,0:T(8,128)}, f32[7,8,1,128]{3,1,2,0:T(8,128)}, u32[]{:S(2)}, u32[]{:S(2)}) collective-permute-start(f32[7,8,1,128]{3,1,2,0:T(8,128)} %bitcast.58), channel_id=1, source_target_pairs={{1,0},{2,1},{3,2},{0,3},{5,4},{6,5},{7,6},{4,7},{9,8},{10,9},{11,1... | collective-permute-start | bytes 86024 | tf_op jit(solution)/shard_map/ppermute | solution.py:49
  44.4 2.3 copy-start.32
  44.4 2.9 %copy-start.38 = (s32[1024]{0:T(1024)S(1)}, s32[1024]{0:T(1024)}, u32[]{:S(2)}) copy-start(s32[1024]{0:T(1024)} %param.22) | copy-start | bytes 12292
  47.5 1.0 copy-start.31
  47.5 1.3 copy-start.34
  47.5 1.3 copy-start.36
  57.5 10.3 %copy-start.29 = (f32[1024]{0:T(1024)}, f32[1024]{0:T(1024)S(1)}, u32[]{:S(2)}) copy-start(f32[1024]{0:T(1024)S(1)} %gather_fusion) | copy-start | bytes 12292
  57.5 2.8 %copy-start.1 = (f32[19,3]{1,0:T(8,128)S(1)}, f32[19,3]{1,0:T(8,128)}, u32[]{:S(2)}) copy-start(f32[19,3]{1,0:T(8,128)} %constant.180.clone) | copy-start | bytes 688
  63.1 7.2 %copy-start.43 = (s32[2]{0:T(128)S(1)}, s32[2]{0:T(128)}, u32[]{:S(2)}) copy-start(s32[2]{0:T(128)} %constant.187) | copy-start | bytes 28
  63.1 7.3 %copy-start.42 = (s32[2]{0:T(128)S(1)}, s32[2]{0:T(128)}, u32[]{:S(2)}) copy-start(s32[2]{0:T(128)} %constant.190) | copy-start | bytes 28
  83.5 104.1 %copy-start.13 = (f32[8,16,1]{2,1,0:T(8,128)S(1)}, f32[8,16,1]{2,1,0:T(8,128)}, u32[]{:S(2)}) copy-start(f32[8,16,1]{2,1,0:T(8,128)} %slice.868) | copy-start | bytes 1540
  83.5 104.2 %copy-start.12 = (f32[8,16,127]{2,1,0:T(8,128)S(1)}, f32[8,16,127]{2,1,0:T(8,128)}, u32[]{:S(2)}) copy-start(f32[8,16,127]{2,1,0:T(8,128)} %slice.870) | copy-start | bytes 195076
  187.6 7.5 %copy-start.20 = (f32[8,16,128]{2,1,0:T(8,128)S(1)}, f32[8,16,128]{2,1,0:T(8,128)}, u32[]{:S(2)}) copy-start(f32[8,16,128]{2,1,0:T(8,128)} %get-tuple-element.81) | copy-start | bytes 196612
  187.6 7.5 %copy-start.21 = (f32[8,16,128]{2,1,0:T(8,128)S(1)}, f32[8,16,128]{2,1,0:T(8,128)}, u32[]{:S(2)}) copy-start(f32[8,16,128]{2,1,0:T(8,128)} %get-tuple-element.82) | copy-start | bytes 196612
  192.5 13.3 %copy-start.27 = (f32[1,8,1,128]{3,1,2,0:T(8,128)}, f32[1,8,1,128]{3,1,2,0:T(8,128)S(1)}, u32[]{:S(2)}) copy-start(f32[1,8,1,128]{3,1,2,0:T(8,128)S(1)} %get-tuple-element.147) | copy-start | bytes 12292
  206.2 1.7 copy-start.4
  206.2 1.7 copy-start.5
  206.2 1.7 copy-start.6
  206.2 1.7 copy-start.7
  207.9 0.9 copy-start.18
  207.9 0.9 copy-start.19
  208.1 0.9 copy-start.8
  208.1 0.9 copy-start.9
  208.1 0.9 copy-start.10
  208.1 0.9 copy-start.11
  212.0 8.6 %copy-start.30 = (f32[1024]{0:T(1024)S(1)}, f32[1024]{0:T(1024)}, u32[]{:S(2)}) copy-start(f32[1024]{0:T(1024)} %copy-done.29) | copy-start | bytes 12292
  212.1 8.6 %copy-start.35 = (f32[1024]{0:T(1024)S(1)}, f32[1024]{0:T(1024)}, u32[]{:S(2)}) copy-start(f32[1024]{0:T(1024)} %get-tuple-element.27) | copy-start | bytes 12292
  212.1 8.6 %copy-start.37 = (pred[1024]{0:T(1024)(128)(4,1)S(1)}, pred[1024]{0:T(1024)(128)(4,1)}, u32[]{:S(2)}) copy-start(pred[1024]{0:T(1024)(128)(4,1)} %get-tuple-element.28) | copy-start | bytes 3076
  212.1 8.7 %copy-start.33 = (s32[1024]{0:T(1024)S(1)}, s32[1024]{0:T(1024)}, u32[]{:S(2)}) copy-start(s32[1024]{0:T(1024)} %broadcast_select_fusion.2) | copy-start | bytes 12292
  226.0 0.7 copy-start.39
  226.0 0.7 copy-start.40
  226.0 0.7 copy-start.41
  226.7 1.0 copy-start.14
  226.7 1.1 copy-start.15
  226.7 1.1 copy-start.16
  226.7 1.1 copy-start.17
  226.7 1.1 copy-start.22
  226.7 1.1 copy-start.23
  226.7 1.1 copy-start.24
  226.7 1.1 copy-start.25
  226.7 1.1 copy-start.26
  226.7 1.1 copy-start.28
  230.5 0.7 copy-start.44
where the time goes:
time: 233 us; the launch traced here: 232 us
  blocking collectives  113 us (48%)
  local copies, waits for them, and re-layouts  58.8 us (25%)
  other arithmetic  31.5 us (14%)
  starting transfers between devices  24.3 us (10%)
  between operations  5.2 us (2%)
    unnamed x1, blocking collectives  104 us
    unnamed x112, local copies, waits for them, and re-layouts  15.5 us
    ppermute x2, starting transfers between devices, padded_2(): lax.ppermute(lax.slice_in_dim(block, 0, width, axis=dim), axis, backward)  15.1 us
    ppermute x2, starting transfers between devices, padded_2(): lax.ppermute(lax.slice_in_dim(block, block.shape[dim] - width, None, axis...  9.21 us
    gather x1, local copies, waits for them, and re-layouts, per_device(): source = flat_post[link_dir, link_site]  8.59 us
    gather x1, local copies, waits for them, and re-layouts, per_device(): current = flat_stream[target, link_site]  8.59 us
    all_gather x1, blocking collectives, per_device(): gathered = lax.all_gather(incoming, 'gy', axis=2, tiled=True)  8.5 us
    scatter-add x1, other arithmetic, per_device(): jax.ops.segment_sum(transfer.T, colloid_slot[link_colloid], num_segments=...  6.8 us
  transfers between devices with their start and end apart: 4, of which 0 were waited for; matrix products, arithmetic and copies ran while one was open for 24% of the time, Pallas kernels for 0%

commit v1 on v0

v1 whole, which is shorter than its diff:
```python
import jax
import jax.numpy as jnp
from jax import lax
from jax.experimental import pallas as pl
from jax.experimental.pallas import tpu as pltpu
from jax.sharding import PartitionSpec as P

VELOCITIES = [
    [0, 0, 0],
    [1, 0, 0],
    [-1, 0, 0],
    [0, 1, 0],
    [0, -1, 0],
    [0, 0, 1],
    [0, 0, -1],
    [1, 1, 0],
    [-1, -1, 0],
    [1, -1, 0],
    [-1, 1, 0],
    [1, 0, 1],
    [-1, 0, -1],
    [1, 0, -1],
    [-1, 0, 1],
    [0, 1, 1],
    [0, -1, -1],
    [0, 1, -1],
    [0, -1, 1],
]
WEIGHTS = [1.0 / 3.0] + [1.0 / 18.0] * 6 + [1.0 / 36.0] * 12
OPPOSITE = [0, 2, 1, 4, 3, 6, 5, 8, 7, 10, 9, 12, 11, 14, 13, 16, 15, 18, 17]
UP_X = [1, 7, 9, 11, 13]
DOWN_X = [2, 8, 10, 12, 14]
UP_Y = [3, 7, 10, 15, 17]
DOWN_Y = [4, 8, 9, 16, 18]
TAU = 0.8
BULK = 0.04
KAPPA = 0.04
MOBILITY = 0.2
PLANE_SPEED = 0.05

MESH = pl.DeviceIdType.MESH
CX, CY, NZ = 8, 16, 128
ROWS = CX * CY
PITCH = 32
NEAR, FAR = 32, 16
F32 = jnp.float32
I32 = jnp.int32


def iota(shape, dim):
    return lax.broadcasted_iota(I32, shape, dim)


def total(terms):
    terms = list(terms)
    while len(terms) > 1:
        terms = [
            terms[i] + terms[i + 1] if i + 1 < len(terms) else terms[i]
            for i in range(0, len(terms), 2)
        ]
    return terms[0]


def signed(values, axis):
    plus = total([values[c] for c in range(19) if VELOCITIES[c][axis] == 1])
    minus = total([values[c] for c in range(19) if VELOCITIES[c][axis] == -1])
    return plus - minus


def lanes_of(table, index):
    return jnp.take_along_axis(table, index, axis=1, mode="promise_in_bounds")


def build_face(pop, phi, out, components, row, phi_rows, change, flag):
    for half in range(2):
        at = pl.ds(row + 8 * half, 8)
        values = [pop[c, at, :] for c in range(19)]
        density = total(values)
        momentum = [signed(values, axis) for axis in range(3)]
        on = jnp.full((8, NZ), flag, I32) == 1
        for slot, c in enumerate(components):
            ex, ey, ez = VELOCITIES[c]
            along = total([e * m for e, m in zip((ex, ey, ez), momentum) if e])
            factor = 3.0 * ey * change + (4.5 * ey * ey - 1.5) * change * change
            correction = factor * density - (3.0 * change) * momentum[1]
            if ey:
                correction = correction + (9.0 * ey * change) * along
            boosted = values[c] + WEIGHTS[c] * correction
            out[slot, pl.ds(8 * half, 8), :] = jnp.where(on, boosted, values[c])
        for slot, phi_row in zip((5, 6), phi_rows):
            out[slot, pl.ds(8 * half, 8), :] = phi[pl.ds(phi_row + 8 * half, 8), :]


def build_rows(pop, phi, out, components, y, phi_ys):
    for slot, c in enumerate(components):
        out[slot] = pop[c, pl.ds(y, 8, stride=CY), :]
    for slot, py in zip((5, 6), phi_ys):
        out[slot] = phi[pl.ds(py, 8, stride=CY), :]


def build_links(pop, site, direction, colloid, count, speed, slots, dmap, wmap, smap, part):
    shape = (8, NZ)
    sub, lane = iota(shape, 0), iota(shape, 1)
    live_to = jnp.zeros(shape, I32)
    for a in range(8):
        live_to = jnp.where(sub == a, count[a], live_to)
    live = lane < live_to
    link_site, link_dir, link_colloid = site[...], direction[...], colloid[...]
    high, low = link_colloid >> 7, link_colloid & 127
    fetched = []
    for table, start in ((speed, 0), (speed, 16), (speed, 32), (slots, 0)):
        value = None
        for h in range(16):
            row = jnp.broadcast_to(table[pl.ds(start + h, 1), :], shape)
            got = lanes_of(row, low)
            value = got if value is None else jnp.where(high == h, got, value)
        fetched.append(value)
    ux, uy, uz, slot = fetched
    steps = []
    for axis in range(3):
        step = jnp.zeros(shape, F32)
        for c in range(1, 19):
            if VELOCITIES[c][axis]:
                step = jnp.where(link_dir == c, float(VELOCITIES[c][axis]), step)
        steps.append(step)
    weight = jnp.where(link_dir < 7, WEIGHTS[1], WEIGHTS[7])
    moved = 6.0 * weight * (steps[0] * ux + steps[1] * uy + steps[2] * uz)
    packed = (link_site & 15) + 16 * jnp.where(live, link_dir, 0)
    for a in range(8):
        packed_row = jnp.broadcast_to(packed[a : a + 1], shape)
        moved_row = jnp.broadcast_to(moved[a : a + 1], shape)
        for half in range(2):
            rows = pl.ds(a * CY + 8 * half, 8)
            index = 8 * (sub + 8 * half) + (lane >> 4)
            code = lanes_of(packed_row, index)
            d = jnp.where((code & 15) == (lane & 15), code >> 4, 0)
            source = jnp.zeros(shape, F32)
            for c in range(1, 19):
                source = jnp.where(d == c, pop[c, rows, :], source)
            dmap[rows, :] = d
            smap[rows, :] = source
            wmap[rows, :] = source - lanes_of(moved_row, index)
    link_z = link_site & 127
    source = jnp.zeros(shape, F32)
    for y in range(CY):
        got = lanes_of(smap[pl.ds(y, 8, stride=CY), :], link_z)
        source = jnp.where((lane >> 3) == y, got, source)
    momentum = jnp.where(live, 2.0 * source - moved, 0.0)
    target = (slot >> 2) & 31
    column = (slot >> 7) * 4 + (slot & 3)
    pieces = [[], [], []]
    for axis in range(3):
        left = steps[axis] * momentum
        for split in range(3):
            piece = left.astype(jnp.bfloat16).astype(F32)
            left = left - piece
            pieces[split].append(piece)
    kind = sub & 3
    left_rows, right_rows = [[], [], []], []
    big = iota((NZ, NZ), 0)
    for a in range(8):
        spread = [
            [jnp.broadcast_to(pieces[s][axis][a : a + 1], shape) for axis in range(3)]
            for s in range(3)
        ]
        pattern = [
            jnp.where(kind == 0, p[0], jnp.where(kind == 1, p[1], jnp.where(kind == 2, p[2], 0.0)))
            for p in spread
        ]
        goes = jnp.broadcast_to(target[a : a + 1], (NZ, NZ)) == (big >> 2)
        for s in range(3):
            full = jnp.broadcast_to(pattern[s][None], (16, 8, NZ)).reshape(NZ, NZ)
            left_rows[s].append(jnp.where(goes, full, 0.0).astype(jnp.bfloat16))
        right_rows.append(
            jnp.where(jnp.broadcast_to(column[a : a + 1], (NZ, NZ)) == big, 1.0, 0.0).astype(
                jnp.bfloat16
            )
        )
    left_matrix = jnp.concatenate([jnp.concatenate(r, axis=1) for r in left_rows], axis=0)
    right_matrix = jnp.concatenate(right_rows, axis=1)
    product = lax.dot_general(
        left_matrix, right_matrix, (((1,), (1,)), ((), ())), preferred_element_type=F32
    )
    product = product[0:NZ] + product[NZ : 2 * NZ] + product[2 * NZ :]
    part[...] = product.reshape(NEAR, 4, NZ)


def prepare(
    pop,
    phi,
    flags,
    site,
    direction,
    colloid,
    count,
    speed,
    slots,
    up_face,
    down_face,
    high_rows,
    low_rows,
    part,
    dmap,
    wmap,
    smap,
):
    gx = lax.axis_index("gx")
    plane_low = flags[gx]
    plane_high = flags[lax.rem(gx + 1, 128)]
    build_face(pop, phi, up_face, UP_X, 112, (96, 112), -PLANE_SPEED, plane_high)
    build_face(pop, phi, down_face, DOWN_X, 0, (0, 16), PLANE_SPEED, plane_low)
    build_rows(pop, phi, high_rows, UP_Y, CY - 1, (CY - 2, CY - 1))
    build_rows(pop, phi, low_rows, DOWN_Y, 0, (0, 1))
    build_links(pop, site, direction, colloid, count, speed, slots, dmap, wmap, smap, part)


def exchange(
    up_face,
    down_face,
    high_rows,
    low_rows,
    part,
    below,
    above,
    south,
    north,
    force,
    near,
    far,
    near_send,
    near_recv,
    far_send,
    far_recv,
    face_send,
    face_recv,
    row_send,
    row_recv,
):
    gx, gy = lax.axis_index("gx"), lax.axis_index("gy")
    slab_up, slab_down = lax.rem(gx + 1, 128), lax.rem(gx + 127, 128)
    near_base = (gx // 8) * 8
    near_me = (gx % 8) * 4 + gy
    far_me = gx // 8
    far_base = gx % 8

    def near_id(k):
        t = lax.rem(near_me + k, NEAR)
        return t, (near_base + t // 4, lax.rem(t, 4))

    def far_id(k):
        h = lax.rem(far_me + k, FAR)
        return h, (h * 8 + far_base, gy)

    barrier = pltpu.get_barrier_semaphore()

    def greet(device):
        pl.semaphore_signal(barrier, inc=1, device_id=device, device_id_type=MESH)

    @pl.loop(1, FAR)
    def _(k):
        greet(far_id(k)[1])

    for slab in (slab_up, slab_down):
        for g in range(4):
            greet((slab, g))

    @pl.loop(1, NEAR)
    def _(k):
        greet(near_id(k)[1])

    pl.semaphore_wait(barrier, FAR - 1 + 8 + NEAR - 1)

    def near_copy(k):
        t, device = near_id(k)
        return pltpu.make_async_remote_copy(
            src_ref=part.at[t],
            dst_ref=near.at[near_me],
            send_sem=near_send.at[t],
            recv_sem=near_recv.at[near_me],
            device_id=device,
            device_id_type=MESH,
        )

    def far_copy(k):
        h, device = far_id(k)
        return pltpu.make_async_remote_copy(
            src_ref=far.at[far_me],
            dst_ref=far.at[far_me],
            send_sem=far_send.at[h],
            recv_sem=far_recv.at[far_me],
            device_id=device,
            device_id_type=MESH,
        )

    rows = pl.ds(pl.multiple_of(gy * CY, CY), CY)
    faces = []
    for side, (src, dst, slab) in enumerate(
        ((up_face, below, slab_up), (down_face, above, slab_down))
    ):
        for g in range(4):
            faces.append(
                pltpu.make_async_remote_copy(
                    src_ref=src,
                    dst_ref=dst.at[:, rows, :],
                    send_sem=face_send.at[side, g],
                    recv_sem=face_recv.at[side, gy],
                    device_id=(slab, g),
                    device_id_type=MESH,
                )
            )
    edges = []
    for side, (src, dst, g) in enumerate(
        ((high_rows, south, lax.rem(gy + 1, 4)), (low_rows, north, lax.rem(gy + 3, 4)))
    ):
        edges.append(
            pltpu.make_async_remote_copy(
                src_ref=src,
                dst_ref=dst,
                send_sem=row_send.at[side],
                recv_sem=row_recv.at[side],
                device_id=(gx, g),
                device_id_type=MESH,
            )
        )

    @pl.loop(1, NEAR)
    def _(k):
        near_copy(k).start()

    for copy in faces:
        copy.start()
    for copy in edges:
        copy.start()

    near[near_me] = part[near_me]

    def arrived(buffer, sem, slot):
        pltpu.make_async_copy(buffer.at[slot], buffer.at[slot], sem.at[slot]).wait()

    @pl.loop(1, NEAR)
    def _(k):
        arrived(near, near_recv, lax.rem(near_me + k, NEAR))

    far[far_me] = total([near[t] for t in range(NEAR)])

    @pl.loop(1, FAR)
    def _(k):
        far_copy(k).start()

    for side, dst in enumerate((below, above)):
        for g in range(4):
            block = dst.at[:, pl.ds(g * CY, CY), :]
            pltpu.make_async_copy(block, block, face_recv.at[side, g]).wait()
    for copy in edges:
        copy.wait_recv()

    @pl.loop(1, FAR)
    def _(k):
        arrived(far, far_recv, lax.rem(far_me + k, FAR))

    summed = total([far[h] for h in range(FAR)])
    force[...] = summed

    for copy in faces + edges:
        copy.wait_send()

    @pl.loop(1, NEAR)
    def _(k):
        near_copy(k).wait_send()

    @pl.loop(1, FAR)
    def _(k):
        far_copy(k).wait_send()


def assemble(pop, phi, below, above, south, north, flags, shift, ext, order):
    gx, gy = lax.axis_index("gx"), lax.axis_index("gy")
    s = shift[0]
    low = s * flags[gx]
    high = s * flags[lax.rem(gx + 1, 128)]
    for x in range(CX):
        own = pl.ds(x * CY, CY)
        order[pl.ds((x + 2) * PITCH + 8, CY), :] = phi[own, :]
        for c in range(19):
            ext[c, pl.ds((x + 1) * PITCH + 8, CY), :] = pop[c, own, :]
    for f in range(7):
        for dst in (below, above):
            for r in range(0, 24, 8):
                dst[f, pl.ds(64 + r, 8), :] = dst[f, pl.ds(r, 8), :]
    begin_low = lax.rem(gy * CY - 2 - low + 128, 64)
    begin_high = lax.rem(gy * CY - 2 + high + 128, 64)
    for src, begin, components, layer, layers in (
        (below, begin_low, UP_X, 0, (0, 1)),
        (above, begin_high, DOWN_X, 9, (10, 11)),
    ):
        for f, c in enumerate(components):
            for k in (0, 8, 10):
                ext[c, pl.ds(layer * PITCH + 7 + k, 8), :] = src[f, pl.ds(begin + 1 + k, 8), :]
        for f, l in zip((5, 6), layers):
            for k in (0, 8, 12):
                order[pl.ds(l * PITCH + 6 + k, 8), :] = src[f, pl.ds(begin + k, 8), :]
    for f in range(5):
        ext[UP_Y[f], pl.ds(PITCH + 7, 8, stride=PITCH), :] = south[f]
        ext[DOWN_Y[f], pl.ds(PITCH + 24, 8, stride=PITCH), :] = north[f]
    order[pl.ds(2 * PITCH + 6, 8, stride=PITCH), :] = south[5]
    order[pl.ds(2 * PITCH + 7, 8, stride=PITCH), :] = south[6]
    order[pl.ds(2 * PITCH + 24, 8, stride=PITCH), :] = north[5]
    order[pl.ds(2 * PITCH + 25, 8, stride=PITCH), :] = north[6]


def turn(value, step):
    return pltpu.roll(value, step % NZ, 1)


def laplace(ref, at):
    centre = ref[pl.ds(at, 8), :]
    return (
        ref[pl.ds(at + PITCH, 8), :]
        + ref[pl.ds(at - PITCH, 8), :]
        + ref[pl.ds(at + 1, 8), :]
        + ref[pl.ds(at - 1, 8), :]
        + turn(centre, -1)
        + turn(centre, 1)
        - 6.0 * centre
    )


def gradient(ref, at):
    centre = ref[pl.ds(at, 8), :]
    return (
        (ref[pl.ds(at + PITCH, 8), :] - ref[pl.ds(at - PITCH, 8), :]) * 0.5,
        (ref[pl.ds(at + 1, 8), :] - ref[pl.ds(at - 1, 8), :]) * 0.5,
        (turn(centre, -1) - turn(centre, 1)) * 0.5,
    )


def collide(ext, order, potential, solid, dmap, wmap, new_pop, new_order):
    @pl.loop(0, CX + 2)
    def _(layer):
        at = pl.multiple_of(layer * PITCH, PITCH)
        for k in (7, 15, 17):
            v = order[pl.ds(at + PITCH + k, 8), :]
            curve = laplace(order, at + PITCH + k)
            potential[pl.ds(at + k, 8), :] = BULK * (v * v * v - v) - KAPPA * curve

    @pl.loop(0, CX)
    def _(x):
        for half in range(2):
            at = pl.multiple_of((x + 1) * PITCH, PITCH) + 8 + 8 * half
            out_rows = pl.ds(pl.multiple_of(x * CY, CY) + 8 * half, 8)
            d = dmap[out_rows, :]
            w = wmap[out_rows, :]
            read = []
            for c in range(19):
                ex, ey, ez = VELOCITIES[c]
                value = ext[c, pl.ds(at - ex * PITCH - ey, 8), :]
                if ez:
                    value = turn(value, ez)
                if c:
                    value = jnp.where(d == OPPOSITE[c], w, value)
                read.append(value)
            phi = order[pl.ds(at + PITCH, 8), :]
            slopes = gradient(potential, at)
            force = [-phi * slope for slope in slopes]
            density = total(read)
            inverse = 1.0 / density
            speed = [(signed(read, axis) + 0.5 * force[axis]) * inverse for axis in range(3)]
            square = speed[0] * speed[0] + speed[1] * speed[1] + speed[2] * speed[2]
            work = speed[0] * force[0] + speed[1] * force[1] + speed[2] * force[2]
            still = solid[out_rows, :] == 1
            half_force = 1.0 - 0.5 / TAU
            base = density * (1.0 / TAU) * (1.0 - 1.5 * square) - (3.0 * half_force) * work
            scaled = density * (1.0 / TAU)
            for c in range(19):
                ex, ey, ez = VELOCITIES[c]
                keep = read[c] * (1.0 - 1.0 / TAU)
                if c == 0:
                    value = keep + WEIGHTS[0] * base
                else:
                    cu = total([e * v for e, v in zip((ex, ey, ez), speed) if e])
                    cf = total([e * v for e, v in zip((ex, ey, ez), force) if e])
                    value = keep + WEIGHTS[c] * (
                        base
                        + scaled * (cu * (3.0 + 4.5 * cu))
                        + (half_force * cf) * (3.0 + 9.0 * cu)
                    )
                new_pop[c, out_rows, :] = jnp.where(still, WEIGHTS[c], value)
            px, py, pz = gradient(order, at + PITCH)
            curve = laplace(potential, at)
            advanced = phi - (speed[0] * px + speed[1] * py + speed[2] * pz) + MOBILITY * curve
            new_order[out_rows, :] = jnp.where(still, phi, advanced)


def finish(
    pop,
    phi,
    solid,
    flags,
    shift,
    below_in,
    above_in,
    south,
    north,
    dmap,
    wmap,
    new_pop,
    new_order,
    below,
    above,
    ext,
    order,
    potential,
):
    below[:, 0:64, :] = below_in[...]
    above[:, 0:64, :] = above_in[...]
    assemble(pop, phi, below, above, south, north, flags, shift, ext, order)
    collide(ext, order, potential, solid, dmap, wmap, new_pop, new_order)


VM = pl.BlockSpec(memory_space=pltpu.VMEM)
SM = pl.BlockSpec(memory_space=pltpu.SMEM)


def shaped(*dims, dtype=F32):
    return jax.ShapeDtypeStruct(dims, dtype)


def per_device(
    populations,
    order_field,
    solid_flags,
    plane_flags,
    shear_shift,
    link_site,
    link_dir,
    link_colloid,
    link_count,
    colloid_slot,
    colloid_speed,
):
    pop = populations.reshape(19, ROWS, NZ)
    phi = order_field.reshape(ROWS, NZ)
    solid = solid_flags.reshape(ROWS, NZ)
    up_face, down_face, high_rows, low_rows, part, dmap, wmap = pl.pallas_call(
        prepare,
        out_shape=(
            shaped(7, CY, NZ),
            shaped(7, CY, NZ),
            shaped(7, 8, NZ),
            shaped(7, 8, NZ),
            shaped(NEAR, 4, NZ),
            shaped(ROWS, NZ, dtype=I32),
            shaped(ROWS, NZ),
        ),
        in_specs=[VM, VM, SM, VM, VM, VM, SM, VM, VM],
        out_specs=[VM] * 7,
        scratch_shapes=[pltpu.VMEM((ROWS, NZ), F32)],
        name="prepare",
    )(
        pop,
        phi,
        plane_flags,
        link_site.reshape(8, NZ),
        link_dir.reshape(8, NZ),
        link_colloid.reshape(8, NZ),
        link_count,
        colloid_speed.reshape(48, NZ),
        colloid_slot.reshape(16, NZ),
    )
    below, above, south, north, force = pl.pallas_call(
        exchange,
        out_shape=(
            shaped(7, 64, NZ),
            shaped(7, 64, NZ),
            shaped(7, 8, NZ),
            shaped(7, 8, NZ),
            shaped(4, NZ),
        ),
        in_specs=[VM] * 5,
        out_specs=[VM] * 5,
        scratch_shapes=[
            pltpu.VMEM((NEAR, 4, NZ), F32),
            pltpu.VMEM((FAR, 4, NZ), F32),
            pltpu.SemaphoreType.DMA((NEAR,)),
            pltpu.SemaphoreType.DMA((NEAR,)),
            pltpu.SemaphoreType.DMA((FAR,)),
            pltpu.SemaphoreType.DMA((FAR,)),
            pltpu.SemaphoreType.DMA((2, 4)),
            pltpu.SemaphoreType.DMA((2, 4)),
            pltpu.SemaphoreType.DMA((2,)),
            pltpu.SemaphoreType.DMA((2,)),
        ],
        compiler_params=pltpu.CompilerParams(collective_id=0, has_side_effects=True),
        name="exchange",
    )(up_face, down_face, high_rows, low_rows, part)
    new_pop, new_order = pl.pallas_call(
        finish,
        out_shape=(shaped(19, ROWS, NZ), shaped(ROWS, NZ)),
        in_specs=[VM, VM, VM, SM, SM] + [VM] * 6,
        out_specs=[VM] * 2,
        scratch_shapes=[
            pltpu.VMEM((7, 88, NZ), F32),
            pltpu.VMEM((7, 88, NZ), F32),
            pltpu.VMEM((19, 10 * PITCH, NZ), F32),
            pltpu.VMEM((12 * PITCH, NZ), F32),
            pltpu.VMEM((10 * PITCH, NZ), F32),
        ],
        name="finish",
    )(
        pop,
        phi,
        solid,
        plane_flags,
        shear_shift,
        below,
        above,
        south,
        north,
        dmap,
        wmap,
    )
    owner = lax.axis_index("gx") // 8
    colloid_force = lax.dynamic_slice(force, (0, owner * 4), (3, 4))
    return (
        new_pop.reshape(populations.shape),
        new_order.reshape(order_field.shape),
        colloid_force,
    )


def solution(mesh):
    return jax.shard_map(
        per_device,
        mesh=mesh,
        in_specs=(
            P(None, "gx", "gy", None),
            P("gx", "gy", None),
            P("gx", "gy", None),
            P(),
            P(),
            P(("gx", "gy")),
            P(("gx", "gy")),
            P(("gx", "gy")),
            P(("gx", "gy")),
            P(),
            P(),
        ),
        out_specs=(P(None, "gx", "gy", None), P("gx", "gy", None), P(None, ("gx", "gy"))),
        check_vma=False,
    )
```

time: 233 us -> 45.6 us (0.20)
  blocking collectives: 113 us -> 0 us
  local copies, waits for them, and re-layouts: 58.8 us -> 2.71 us
  Pallas kernels: 0 us -> 41.3 us
  other arithmetic: 31.5 us -> 0 us
  starting transfers between devices: 24.3 us -> 0 us
  between operations: 5.2 us -> 1.31 us
    unnamed x1 -> x0, blocking collectives: 104 us -> none
    pallas_call x0 -> x3, Pallas kernels: none -> 41.3 us  [the longest x1 33.5 us: per_device(): pl.pallas_call(exchange, out_shape=(shaped(7, 64, NZ), shaped(7, 64, NZ),...]
    gather x6 -> x0, local copies, waits for them, and re-layouts: 29.6 us -> none  [the longest x1 8.59 us: per_device(): source = flat_post[link_dir, link_site]]
    ppermute x4 -> x0, starting transfers between devices: 24.3 us -> none  [the longest x2 15.1 us: padded_2(): lax.ppermute(lax.slice_in_dim(block, 0, width, axis=dim), axis, backward)]
    unnamed x112 -> x0, local copies, waits for them, and re-layouts: 15.5 us -> none
    all_gather x1 -> x0, blocking collectives: 8.5 us -> none  [per_device(): gathered = lax.all_gather(incoming, 'gy', axis=2, tiled=True)]
    slice x26 -> x0, local copies, waits for them, and re-layouts: 7.14 us -> none  [the longest x10 1.78 us: per_device(): pieces.append(jnp.roll(pulled, upward_step, 2))]
    scatter-add x1 -> x0, other arithmetic: 6.8 us -> none  [per_device(): jax.ops.segment_sum(transfer.T, colloid_slot[link_colloid], num_segments=...]
  transfers between devices with their start and end apart: 4 -> 0, of which waited for: 0 -> 0; matrix products, arithmetic and copies ran while one was open for 24% -> 0% of each run, Pallas kernels for 0% -> 0%
where the time goes in v1:
time: 45.6 us; the launch traced here: 45.3 us
  Pallas kernels  41.3 us (91%)
  local copies, waits for them, and re-layouts  2.71 us (6%)
  between operations  1.31 us (3%)
    pallas_call x1, Pallas kernels, per_device(): pl.pallas_call(exchange, out_shape=(shaped(7, 64, NZ), shaped(7, 64, NZ),...  33.5 us
    pallas_call x1, Pallas kernels, per_device(): pl.pallas_call(finish, out_shape=(shaped(19, ROWS, NZ), shaped(ROWS, NZ))...  5.08 us
    pallas_call x1, Pallas kernels, per_device(): pl.pallas_call(prepare, out_shape=(shaped(7, CY, NZ), shaped(7, CY, NZ),...  2.66 us
    reshape x1, local copies, waits for them, and re-layouts, per_device(): colloid_speed.reshape(48, NZ)  1.39 us
    dynamic_slice x1, local copies, waits for them, and re-layouts, per_device(): colloid_force = lax.dynamic_slice(force, (0, owner * 4), (3, 4))  1.32 us

profile of v1, /device:TPU:1, one launch (start us, length us, event | category | flops | bytes accessed | tf_op | source)
XLA Modules:
  0.0 45.3 jit_solution(8858987322758951131)
XLA Ops:
  1.3 1.4 %reshape.42.speed = f32[48,128]{1,0:T(8,128)} reshape(f32[3,2048]{1,0:T(4,128)} %param.21) | data formatting | bytes 49152 | tf_op jit(solution)/shard_map/reshape | solution.py:567
  2.7 2.7 %prepare.1 = (f32[7,16,128]{2,1,0:T(8,128)}, f32[7,16,128]{2,1,0:T(8,128)}, f32[7,8,128]{2,1,0:T(8,128)}, f32[7,8,128]{2,1,0:T(8,128)}, f32[32,4,128]{2,1,0:T(4,...) custom-call(f32[19,128,128]{2,1,0:T(8,128)} %bitcast.9, f32[128,128]{1,0:T(8,128)} %bitcast.11, s32[128]{0:T(128)} %flags.3, ...), custom_call_target="tpu_custom_call" | custom-call | tf_op jit(solution)/shard_map/prepare/pallas_call | solution.py:544
  5.3 33.5 %exchange.1 = (f32[7,64,128]{2,1,0:T(8,128)}, f32[7,64,128]{2,1,0:T(8,128)}, f32[7,8,128]{2,1,0:T(8,128)}, f32[7,8,128]{2,1,0:T(8,128)}, f32[4,128]{1,0:T(4,128)}) custom-call(f32[7,16,128]{2,1,0:T(8,128)} %get-tuple-element.17.up_face, f32[7,16,128]{2,1,0:T(8,128)} %get-tuple-element.18.down_face, f32[7,8,128]{2,1,0:T(8,128)} %get-tuple-element.19.high_rows, ...), custom_call_target="tpu_custom_call" | custom-call | tf_op jit(solution)/shard_map/exchange/pallas_call | solution.py:570
  38.9 1.3 %constant_dynamic-slice_fusion = f32[3,4]{1,0:T(4,128)} fusion(f32[4,128]{1,0:T(4,128)} %get-tuple-element.30, s32[]{:T(128)S(6)} %select_n.9), kind=kLoop, calls=%fused_computation | loop fusion | bytes 100 | tf_op jit(solution)/shard_map/dynamic_slice | solution.py:623
  40.2 5.1 %finish.1 = (f32[19,128,128]{2,1,0:T(8,128)}, f32[128,128]{1,0:T(8,128)}) custom-call(f32[19,128,128]{2,1,0:T(8,128)} %bitcast.10, f32[128,128]{1,0:T(8,128)} %bitcast.12, s32[128,128]{1,0:T(8,128)} %bitcast.13, s32[128]{0:T(128)} %flags.3, s32[1]{0:T(128)S(6)} %copy.14.shift, f32[7,64,128]{2,1,0:T(8,128)} %get-tuple-element.22.below_in, ...), custom_call_target="tpu_custom_call" | custom-call | tf_op jit(solution)/shard_map/finish/pallas_call | solution.py:596

commit v2 on v1

v2 whole, which is shorter than its diff:
```python
import jax
import jax.numpy as jnp
from jax import lax
from jax.experimental import pallas as pl
from jax.experimental.pallas import tpu as pltpu
from jax.sharding import PartitionSpec as P

VELOCITIES = [
    [0, 0, 0],
    [1, 0, 0],
    [-1, 0, 0],
    [0, 1, 0],
    [0, -1, 0],
    [0, 0, 1],
    [0, 0, -1],
    [1, 1, 0],
    [-1, -1, 0],
    [1, -1, 0],
    [-1, 1, 0],
    [1, 0, 1],
    [-1, 0, -1],
    [1, 0, -1],
    [-1, 0, 1],
    [0, 1, 1],
    [0, -1, -1],
    [0, 1, -1],
    [0, -1, 1],
]
WEIGHTS = [1.0 / 3.0] + [1.0 / 18.0] * 6 + [1.0 / 36.0] * 12
OPPOSITE = [0, 2, 1, 4, 3, 6, 5, 8, 7, 10, 9, 12, 11, 14, 13, 16, 15, 18, 17]
UP_X = [1, 7, 9, 11, 13]
DOWN_X = [2, 8, 10, 12, 14]
UP_Y = [3, 7, 10, 15, 17]
DOWN_Y = [4, 8, 9, 16, 18]
TAU = 0.8
BULK = 0.04
KAPPA = 0.04
MOBILITY = 0.2
PLANE_SPEED = 0.05

MESH = pl.DeviceIdType.MESH
CX, CY, NZ = 8, 16, 128
ROWS = CX * CY
PITCH = 32
NEAR, FAR = 32, 16
F32 = jnp.float32
I32 = jnp.int32


def iota(shape, dim):
    return lax.broadcasted_iota(I32, shape, dim)


def total(terms):
    terms = list(terms)
    while len(terms) > 1:
        terms = [
            terms[i] + terms[i + 1] if i + 1 < len(terms) else terms[i]
            for i in range(0, len(terms), 2)
        ]
    return terms[0]


def signed(values, axis):
    plus = total([values[c] for c in range(19) if VELOCITIES[c][axis] == 1])
    minus = total([values[c] for c in range(19) if VELOCITIES[c][axis] == -1])
    return plus - minus


def lanes_of(table, index):
    return jnp.take_along_axis(table, index, axis=1, mode="promise_in_bounds")


def build_face(pop, phi, out, components, row, phi_rows, change, flag):
    for half in range(2):
        at = pl.ds(row + 8 * half, 8)
        values = [pop[c, at, :] for c in range(19)]
        density = total(values)
        momentum = [signed(values, axis) for axis in range(3)]
        on = jnp.full((8, NZ), flag, I32) == 1
        for slot, c in enumerate(components):
            ex, ey, ez = VELOCITIES[c]
            along = total([e * m for e, m in zip((ex, ey, ez), momentum) if e])
            factor = 3.0 * ey * change + (4.5 * ey * ey - 1.5) * change * change
            correction = factor * density - (3.0 * change) * momentum[1]
            if ey:
                correction = correction + (9.0 * ey * change) * along
            boosted = values[c] + WEIGHTS[c] * correction
            out[slot, pl.ds(8 * half, 8), :] = jnp.where(on, boosted, values[c])
        for slot, phi_row in zip((5, 6), phi_rows):
            out[slot, pl.ds(8 * half, 8), :] = phi[pl.ds(phi_row + 8 * half, 8), :]


def build_rows(pop, phi, out, components, y, phi_ys):
    for slot, c in enumerate(components):
        out[slot] = pop[c, pl.ds(PITCH + 8 + y, 8, stride=PITCH), :]
    for slot, py in zip((5, 6), phi_ys):
        out[slot] = phi[pl.ds(py, 8, stride=CY), :]


def build_links(pop, site, direction, colloid, count, speed, slots, dmap, wmap, smap, part):
    shape = (8, NZ)
    sub, lane = iota(shape, 0), iota(shape, 1)
    live_to = jnp.zeros(shape, I32)
    for a in range(8):
        live_to = jnp.where(sub == a, count[a], live_to)
    live = lane < live_to
    link_site, link_dir, link_colloid = site[...], direction[...], colloid[...]
    high, low = link_colloid >> 7, link_colloid & 127
    fetched = []
    for axis in range(4):
        value = None
        for h in range(16):
            if axis < 3:
                row = speed[pl.ds(axis, 1), pl.ds(h * NZ, NZ)]
            else:
                row = slots[pl.ds(h, 1), :]
            row = jnp.broadcast_to(row, shape)
            got = lanes_of(row, low)
            value = got if value is None else jnp.where(high == h, got, value)
        fetched.append(value)
    ux, uy, uz, slot = fetched
    steps = []
    for axis in range(3):
        step = jnp.zeros(shape, F32)
        for c in range(1, 19):
            if VELOCITIES[c][axis]:
                step = jnp.where(link_dir == c, float(VELOCITIES[c][axis]), step)
        steps.append(step)
    weight = jnp.where(link_dir < 7, WEIGHTS[1], WEIGHTS[7])
    moved = 6.0 * weight * (steps[0] * ux + steps[1] * uy + steps[2] * uz)
    packed = (link_site & 15) + 16 * jnp.where(live, link_dir, 0)
    for a in range(8):
        packed_row = jnp.broadcast_to(packed[a : a + 1], shape)
        moved_row = jnp.broadcast_to(moved[a : a + 1], shape)
        for half in range(2):
            rows = pl.ds(a * CY + 8 * half, 8)
            index = 8 * (sub + 8 * half) + (lane >> 4)
            code = lanes_of(packed_row, index)
            d = jnp.where((code & 15) == (lane & 15), code >> 4, 0)
            source = jnp.zeros(shape, F32)
            for c in range(1, 19):
                source = jnp.where(d == c, pop[c, pl.ds((a + 1) * PITCH + 8 + 8 * half, 8), :], source)
            dmap[rows, :] = d
            smap[rows, :] = source
            wmap[rows, :] = source - lanes_of(moved_row, index)
    link_z = link_site & 127
    source = jnp.zeros(shape, F32)
    for y in range(CY):
        got = lanes_of(smap[pl.ds(y, 8, stride=CY), :], link_z)
        source = jnp.where((lane >> 3) == y, got, source)
    momentum = jnp.where(live, 2.0 * source - moved, 0.0)
    target = (slot >> 10) * 16 + ((slot >> 2) & 15)
    column = ((slot >> 6) & 15) * 4 + (slot & 3)
    pieces = [[], [], []]
    for axis in range(3):
        left = steps[axis] * momentum
        for split in range(3):
            piece = left.astype(jnp.bfloat16).astype(F32)
            left = left - piece
            pieces[split].append(piece)
    kind = sub & 3
    left_rows, right_rows = [[], [], []], []
    big = iota((NZ, NZ), 0)
    for a in range(8):
        spread = [
            [jnp.broadcast_to(pieces[s][axis][a : a + 1], shape) for axis in range(3)]
            for s in range(3)
        ]
        pattern = [
            jnp.where(kind == 0, p[0], jnp.where(kind == 1, p[1], jnp.where(kind == 2, p[2], 0.0)))
            for p in spread
        ]
        goes = jnp.broadcast_to(target[a : a + 1], (NZ, NZ)) == (big >> 2)
        for s in range(3):
            full = jnp.broadcast_to(pattern[s][None], (16, 8, NZ)).reshape(NZ, NZ)
            left_rows[s].append(jnp.where(goes, full, 0.0).astype(jnp.bfloat16))
        right_rows.append(
            jnp.where(jnp.broadcast_to(column[a : a + 1], (NZ, NZ)) == big, 1.0, 0.0).astype(
                jnp.bfloat16
            )
        )
    left_matrix = jnp.concatenate([jnp.concatenate(r, axis=1) for r in left_rows], axis=0)
    right_matrix = jnp.concatenate(right_rows, axis=1)
    product = lax.dot_general(
        left_matrix, right_matrix, (((1,), (1,)), ((), ())), preferred_element_type=F32
    )
    product = product[0:NZ] + product[NZ : 2 * NZ] + product[2 * NZ :]
    part[...] = product.reshape(NEAR, 4, NZ)


def turn(value, step):
    return pltpu.roll(value, step % NZ, 1)


def laplace(ref, at):
    centre = ref[pl.ds(at, 8), :]
    return (
        ref[pl.ds(at + PITCH, 8), :]
        + ref[pl.ds(at - PITCH, 8), :]
        + ref[pl.ds(at + 1, 8), :]
        + ref[pl.ds(at - 1, 8), :]
        + turn(centre, -1)
        + turn(centre, 1)
        - 6.0 * centre
    )


def gradient(ref, at):
    centre = ref[pl.ds(at, 8), :]
    return (
        (ref[pl.ds(at + PITCH, 8), :] - ref[pl.ds(at - PITCH, 8), :]) * 0.5,
        (ref[pl.ds(at + 1, 8), :] - ref[pl.ds(at - 1, 8), :]) * 0.5,
        (turn(centre, -1) - turn(centre, 1)) * 0.5,
    )


def collide(ext, order, potential, solid, dmap, wmap, new_pop, new_order):
    @pl.loop(0, CX + 2)
    def _(layer):
        at = pl.multiple_of(layer * PITCH, PITCH)
        for k in (7, 15, 17):
            v = order[pl.ds(at + PITCH + k, 8), :]
            curve = laplace(order, at + PITCH + k)
            potential[pl.ds(at + k, 8), :] = BULK * (v * v * v - v) - KAPPA * curve

    @pl.loop(0, CX)
    def _(x):
        for half in range(2):
            at = pl.multiple_of((x + 1) * PITCH, PITCH) + 8 + 8 * half
            out_rows = pl.ds(pl.multiple_of(x * CY, CY) + 8 * half, 8)
            d = dmap[out_rows, :]
            w = wmap[out_rows, :]
            read = []
            for c in range(19):
                ex, ey, ez = VELOCITIES[c]
                value = ext[c, pl.ds(at - ex * PITCH - ey, 8), :]
                if ez:
                    value = turn(value, ez)
                if c:
                    value = jnp.where(d == OPPOSITE[c], w, value)
                read.append(value)
            phi = order[pl.ds(at + PITCH, 8), :]
            slopes = gradient(potential, at)
            force = [-phi * slope for slope in slopes]
            density = total(read)
            inverse = 1.0 / density
            speed = [(signed(read, axis) + 0.5 * force[axis]) * inverse for axis in range(3)]
            square = speed[0] * speed[0] + speed[1] * speed[1] + speed[2] * speed[2]
            work = speed[0] * force[0] + speed[1] * force[1] + speed[2] * force[2]
            still = solid[out_rows, :] == 1
            half_force = 1.0 - 0.5 / TAU
            base = density * (1.0 / TAU) * (1.0 - 1.5 * square) - (3.0 * half_force) * work
            scaled = density * (1.0 / TAU)
            for c in range(19):
                ex, ey, ez = VELOCITIES[c]
                keep = read[c] * (1.0 - 1.0 / TAU)
                if c == 0:
                    value = keep + WEIGHTS[0] * base
                else:
                    cu = total([e * v for e, v in zip((ex, ey, ez), speed) if e])
                    cf = total([e * v for e, v in zip((ex, ey, ez), force) if e])
                    value = keep + WEIGHTS[c] * (
                        base
                        + scaled * (cu * (3.0 + 4.5 * cu))
                        + (half_force * cf) * (3.0 + 9.0 * cu)
                    )
                new_pop[c, out_rows, :] = jnp.where(still, WEIGHTS[c], value)
            px, py, pz = gradient(order, at + PITCH)
            curve = laplace(potential, at)
            advanced = phi - (speed[0] * px + speed[1] * py + speed[2] * pz) + MOBILITY * curve
            new_order[out_rows, :] = jnp.where(still, phi, advanced)


def step(
    pop,
    phi,
    solid,
    flags,
    shift,
    site,
    direction,
    colloid,
    count,
    speed,
    slots,
    new_pop,
    new_order,
    force,
    ext,
    order,
    potential,
    out,
    below,
    above,
    south,
    north,
    up_face,
    down_face,
    high_rows,
    low_rows,
    part,
    near,
    far,
    dmap,
    wmap,
    smap,
    in_sem,
    out_sem,
    near_send,
    near_recv,
    far_send,
    far_recv,
    face_send,
    face_recv,
    row_send,
    row_recv,
):
    gx, gy = lax.axis_index("gx"), lax.axis_index("gy")
    slab_up, slab_down = lax.rem(gx + 1, 128), lax.rem(gx + 127, 128)
    z, y, x_lo = lax.rem(gx // 4, 16), lax.rem(gx, 4), gx // 64
    near_me = x_lo * 16 + y * 4 + gy

    def near_id(k):
        t = lax.rem(near_me + k, NEAR)
        return t, ((t // 16) * 64 + z * 4 + lax.rem(t // 4, 4), lax.rem(t, 4))

    def far_id(k):
        h = lax.rem(z + k, FAR)
        return h, (x_lo * 64 + h * 4 + y, gy)

    barrier = pltpu.get_barrier_semaphore()

    def greet(device):
        pl.semaphore_signal(barrier, inc=1, device_id=device, device_id_type=MESH)

    @pl.loop(1, FAR)
    def _(k):
        greet(far_id(k)[1])

    for slab in (slab_up, slab_down):
        for g in range(4):
            greet((slab, g))

    @pl.loop(1, NEAR)
    def _(k):
        greet(near_id(k)[1])

    loads = [
        pltpu.make_async_copy(
            pop.at[:, pl.ds(x * CY, CY), :],
            ext.at[:, pl.ds((x + 1) * PITCH + 8, CY), :],
            in_sem.at[x],
        )
        for x in range(CX)
    ]
    for x in (0, 7, 1, 2, 3, 4, 5, 6):
        loads[x].start()
    for x in range(CX):
        order[pl.ds((x + 2) * PITCH + 8, CY), :] = phi[pl.ds(x * CY, CY), :]
    plane_low = flags[gx]
    plane_high = flags[slab_up]
    for x in range(CX):
        loads[x].wait()
    first, last = PITCH + 8, 8 * PITCH + 8
    build_face(ext, phi, up_face, UP_X, last, (96, 112), -PLANE_SPEED, plane_high)
    build_face(ext, phi, down_face, DOWN_X, first, (0, 16), PLANE_SPEED, plane_low)
    build_rows(ext, phi, high_rows, UP_Y, CY - 1, (CY - 2, CY - 1))
    build_rows(ext, phi, low_rows, DOWN_Y, 0, (0, 1))
    build_links(ext, site, direction, colloid, count, speed, slots, dmap, wmap, smap, part)

    pl.semaphore_wait(barrier, FAR - 1 + 8 + NEAR - 1)

    def near_copy(k):
        t, device = near_id(k)
        return pltpu.make_async_remote_copy(
            src_ref=part.at[t],
            dst_ref=near.at[near_me],
            send_sem=near_send.at[t],
            recv_sem=near_recv.at[near_me],
            device_id=device,
            device_id_type=MESH,
        )

    def far_copy(k):
        h, device = far_id(k)
        return pltpu.make_async_remote_copy(
            src_ref=far.at[z],
            dst_ref=far.at[z],
            send_sem=far_send.at[h],
            recv_sem=far_recv.at[z],
            device_id=device,
            device_id_type=MESH,
        )

    rows = pl.ds(pl.multiple_of(gy * CY, CY), CY)
    faces = []
    for side, (src, dst, slab) in enumerate(
        ((up_face, below, slab_up), (down_face, above, slab_down))
    ):
        for g in range(4):
            faces.append(
                pltpu.make_async_remote_copy(
                    src_ref=src,
                    dst_ref=dst.at[:, rows, :],
                    send_sem=face_send.at[side, g],
                    recv_sem=face_recv.at[side, gy],
                    device_id=(slab, g),
                    device_id_type=MESH,
                )
            )
    edges = []
    for side, (src, dst, g) in enumerate(
        ((high_rows, south, lax.rem(gy + 1, 4)), (low_rows, north, lax.rem(gy + 3, 4)))
    ):
        edges.append(
            pltpu.make_async_remote_copy(
                src_ref=src,
                dst_ref=dst,
                send_sem=row_send.at[side],
                recv_sem=row_recv.at[side],
                device_id=(gx, g),
                device_id_type=MESH,
            )
        )

    @pl.loop(1, NEAR)
    def _(k):
        near_copy(k).start()

    for copy in faces:
        copy.start()
    for copy in edges:
        copy.start()

    near[near_me] = part[near_me]

    def arrived(buffer, sem, slot):
        pltpu.make_async_copy(buffer.at[slot], buffer.at[slot], sem.at[slot]).wait()

    @pl.loop(1, NEAR)
    def _(k):
        arrived(near, near_recv, lax.rem(near_me + k, NEAR))

    far[z] = total([near[t] for t in range(NEAR)])

    @pl.loop(1, FAR)
    def _(k):
        far_copy(k).start()

    for copy in edges:
        copy.wait_recv()
    for f in range(5):
        ext[UP_Y[f], pl.ds(PITCH + 7, 8, stride=PITCH), :] = south[f]
        ext[DOWN_Y[f], pl.ds(PITCH + 24, 8, stride=PITCH), :] = north[f]
    order[pl.ds(2 * PITCH + 6, 8, stride=PITCH), :] = south[5]
    order[pl.ds(2 * PITCH + 7, 8, stride=PITCH), :] = south[6]
    order[pl.ds(2 * PITCH + 24, 8, stride=PITCH), :] = north[5]
    order[pl.ds(2 * PITCH + 25, 8, stride=PITCH), :] = north[6]

    for side, dst in enumerate((below, above)):
        for g in range(4):
            block = dst.at[:, pl.ds(g * CY, CY), :]
            pltpu.make_async_copy(block, block, face_recv.at[side, g]).wait()

    for f in range(7):
        for dst in (below, above):
            for r in range(0, 24, 8):
                dst[f, pl.ds(64 + r, 8), :] = dst[f, pl.ds(r, 8), :]
    s = shift[0]
    begin_low = lax.rem(gy * CY - 2 - s * plane_low + 128, 64)
    begin_high = lax.rem(gy * CY - 2 + s * plane_high + 128, 64)
    for src, begin, components, layer, layers in (
        (below, begin_low, UP_X, 0, (0, 1)),
        (above, begin_high, DOWN_X, 9, (10, 11)),
    ):
        for f, c in enumerate(components):
            for k in (0, 8, 10):
                ext[c, pl.ds(layer * PITCH + 7 + k, 8), :] = src[f, pl.ds(begin + 1 + k, 8), :]
        for f, l in zip((5, 6), layers):
            for k in (0, 8, 12):
                order[pl.ds(l * PITCH + 6 + k, 8), :] = src[f, pl.ds(begin + k, 8), :]

    collide(ext, order, potential, solid, dmap, wmap, out, new_order)
    stores = [
        pltpu.make_async_copy(out.at[:, pl.ds(x * CY, CY), :], new_pop.at[:, pl.ds(x * CY, CY), :], out_sem.at[x])
        for x in range(CX)
    ]
    for copy in stores:
        copy.start()

    @pl.loop(1, FAR)
    def _(k):
        arrived(far, far_recv, lax.rem(z + k, FAR))

    summed = total([far[h] for h in range(FAR)])
    force[...] = pltpu.roll(summed, lax.rem(NZ - 4 * z, NZ), 1)[0:3, 0:4]

    for copy in stores:
        copy.wait()
    for copy in faces + edges:
        copy.wait_send()

    @pl.loop(1, NEAR)
    def _(k):
        near_copy(k).wait_send()

    @pl.loop(1, FAR)
    def _(k):
        far_copy(k).wait_send()


VM = pl.BlockSpec(memory_space=pltpu.VMEM)
SM = pl.BlockSpec(memory_space=pltpu.SMEM)
HB = pl.BlockSpec(memory_space=pl.ANY)


def shaped(*dims, dtype=F32):
    return jax.ShapeDtypeStruct(dims, dtype)


def per_device(
    populations,
    order_field,
    solid_flags,
    plane_flags,
    shear_shift,
    link_site,
    link_dir,
    link_colloid,
    link_count,
    colloid_slot,
    colloid_speed,
):
    new_pop, new_order, force = pl.pallas_call(
        step,
        out_shape=(shaped(19, ROWS, NZ), shaped(ROWS, NZ), shaped(3, 4)),
        in_specs=[HB, VM, VM, SM, SM, VM, VM, VM, SM, VM, VM],
        out_specs=[HB, VM, VM],
        scratch_shapes=[
            pltpu.VMEM((19, 10 * PITCH, NZ), F32),
            pltpu.VMEM((12 * PITCH, NZ), F32),
            pltpu.VMEM((10 * PITCH, NZ), F32),
            pltpu.VMEM((19, ROWS, NZ), F32),
            pltpu.VMEM((7, 88, NZ), F32),
            pltpu.VMEM((7, 88, NZ), F32),
            pltpu.VMEM((7, 8, NZ), F32),
            pltpu.VMEM((7, 8, NZ), F32),
            pltpu.VMEM((7, CY, NZ), F32),
            pltpu.VMEM((7, CY, NZ), F32),
            pltpu.VMEM((7, 8, NZ), F32),
            pltpu.VMEM((7, 8, NZ), F32),
            pltpu.VMEM((NEAR, 4, NZ), F32),
            pltpu.VMEM((NEAR, 4, NZ), F32),
            pltpu.VMEM((FAR, 4, NZ), F32),
            pltpu.VMEM((ROWS, NZ), I32),
            pltpu.VMEM((ROWS, NZ), F32),
            pltpu.VMEM((ROWS, NZ), F32),
            pltpu.SemaphoreType.DMA((CX,)),
            pltpu.SemaphoreType.DMA((CX,)),
            pltpu.SemaphoreType.DMA((NEAR,)),
            pltpu.SemaphoreType.DMA((NEAR,)),
            pltpu.SemaphoreType.DMA((FAR,)),
            pltpu.SemaphoreType.DMA((FAR,)),
            pltpu.SemaphoreType.DMA((2, 4)),
            pltpu.SemaphoreType.DMA((2, 4)),
            pltpu.SemaphoreType.DMA((2,)),
            pltpu.SemaphoreType.DMA((2,)),
        ],
        compiler_params=pltpu.CompilerParams(collective_id=0, has_side_effects=True),
        name="step",
    )(
        populations.reshape(19, ROWS, NZ),
        order_field.reshape(ROWS, NZ),
        solid_flags.reshape(ROWS, NZ),
        plane_flags,
        shear_shift,
        link_site.reshape(8, NZ),
        link_dir.reshape(8, NZ),
        link_colloid.reshape(8, NZ),
        link_count,
        colloid_speed,
        colloid_slot.reshape(16, NZ),
    )
    return new_pop.reshape(populations.shape), new_order.reshape(order_field.shape), force


def solution(mesh):
    return jax.shard_map(
        per_device,
        mesh=mesh,
        in_specs=(
            P(None, "gx", "gy", None),
            P("gx", "gy", None),
            P("gx", "gy", None),
            P(),
            P(),
            P(("gx", "gy")),
            P(("gx", "gy")),
            P(("gx", "gy")),
            P(("gx", "gy")),
            P(),
            P(),
        ),
        out_specs=(P(None, "gx", "gy", None), P("gx", "gy", None), P(None, ("gx", "gy"))),
        check_vma=False,
    )
```

time: 45.6 us -> 39.6 us (0.87)
  Pallas kernels: 41.3 us -> 34.1 us
  local copies, waits for them, and re-layouts: 2.71 us -> 3.69 us
    pallas_call x3 -> x1, Pallas kernels: 41.3 us -> 34.1 us  [per_device(): pl.pallas_call(step, out_shape=(shaped(19, ROWS, NZ), shaped(ROWS, NZ), s...]
    unnamed x0 -> x7, local copies, waits for them, and re-layouts: none -> 3.69 us
    reshape x1 -> x0, local copies, waits for them, and re-layouts: 1.39 us -> none  [per_device(): colloid_speed.reshape(48, NZ)]
    dynamic_slice x1 -> x0, local copies, waits for them, and re-layouts: 1.32 us -> none  [per_device(): colloid_force = lax.dynamic_slice(force, (0, owner * 4), (3, 4))]
where the time goes in v2:
time: 39.6 us; the launch traced here: 39.1 us
  Pallas kernels  34.1 us (86%)
  local copies, waits for them, and re-layouts  3.69 us (9%)
  between operations  1.31 us (3%)
    pallas_call x1, Pallas kernels, per_device(): pl.pallas_call(step, out_shape=(shaped(19, ROWS, NZ), shaped(ROWS, NZ), s...  34.1 us
    unnamed x7, local copies, waits for them, and re-layouts  3.69 us

profile of v2, /device:TPU:1, one launch (start us, length us, event | category | flops | bytes accessed | tf_op | source)
XLA Modules:
  0.0 39.1 jit_solution(1189367742338437648)
XLA Ops:
  1.3 34.1 %step.1 = (f32[19,128,128]{2,1,0:T(8,128)}, f32[128,128]{1,0:T(8,128)}, f32[3,4]{1,0:T(4,128)}) custom-call(f32[19,128,128]{2,1,0:T(8,128)} %bitcast.9, f32[128,128]{1,0:T(8,128)} %bitcast.11, s32[128,128]{1,0:T(8,128)} %bitcast.12, s32[128]{0:T(128)} %flags.1, s32[1]{0:T(128)S(6)} %copy.17.shift, s32[8,128]{1,0:T(8,128)} %bitcast.15, s32[8,128]{1,0:T(8,128)} %bitcast.16, ...), custom_call_target="tpu_custom_call" | custom-call | tf_op jit(solution)/shard_map/step/pallas_call | solution.py:535
  35.4 0.0 copy-start
  35.4 0.0 copy-start.1
  35.4 2.5 %copy.18 = f32[19,8,16,128]{3,2,1,0:T(8,128)} copy(f32[19,8,16,128]{3,2,1,0:T(8,128)} %bitcast.10) | data formatting | bytes 2490368
  37.9 0.0 copy-done
  37.9 0.6 %copy.19 = f32[8,16,128]{2,1,0:T(8,128)} copy(f32[8,16,128]{2,1,0:T(8,128)S(1)} %bitcast.13) | data formatting | bytes 131072
  38.5 0.0 copy-done.1
  38.5 0.6 %copy.20 = f32[3,4]{1,0:T(4,128)} copy(f32[3,4]{1,0:T(4,128)S(1)} %copy-done.1) | data formatting | bytes 96
Async XLA Ops:
  35.4 2.5 %copy-start = (f32[128,128]{1,0:T(8,128)S(1)}, f32[128,128]{1,0:T(8,128)}, u32[]{:S(2)}) copy-start(f32[128,128]{1,0:T(8,128)} %get-tuple-element.7) | copy-start | bytes 196612
  35.4 3.1 %copy-start.1 = (f32[3,4]{1,0:T(4,128)S(1)}, f32[3,4]{1,0:T(4,128)}, u32[]{:S(2)}) copy-start(f32[3,4]{1,0:T(4,128)} %get-tuple-element.14) | copy-start | bytes 148

commit v3 on v2

--- a/solution.py
+++ b/solution.py
@@ -274,6 +274,19 @@
 
 def step(
     pop,
+    phi_in,
+    solid_in,
+    flags_in,
+    shift_in,
+    site_in,
+    direction_in,
+    colloid_in,
+    count_in,
+    speed_in,
+    slots_in,
+    out,
+    new_order,
+    force,
     phi,
     solid,
     flags,
@@ -284,13 +297,9 @@
     count,
     speed,
     slots,
-    new_pop,
-    new_order,
-    force,
     ext,
     order,
     potential,
-    out,
     below,
     above,
     south,
@@ -306,7 +315,6 @@
     wmap,
     smap,
     in_sem,
-    out_sem,
     near_send,
     near_recv,
     far_send,
@@ -320,6 +328,7 @@
     slab_up, slab_down = lax.rem(gx + 1, 128), lax.rem(gx + 127, 128)
     z, y, x_lo = lax.rem(gx // 4, 16), lax.rem(gx, 4), gx // 64
     near_me = x_lo * 16 + y * 4 + gy
+    core = lax.rem(gy, 2)
 
     def near_id(k):
         t = lax.rem(near_me + k, NEAR)
@@ -339,8 +348,8 @@
         greet(far_id(k)[1])
 
     for slab in (slab_up, slab_down):
-        for g in range(4):
-            greet((slab, g))
+        for chip in range(2):
+            greet((slab, 2 * chip + core))
 
     @pl.loop(1, NEAR)
     def _(k):
@@ -354,8 +363,29 @@
         )
         for x in range(CX)
     ]
+    small = [
+        pltpu.make_async_copy(source, target, in_sem.at[CX + i])
+        for i, (source, target) in enumerate(
+            (
+                (site_in, site),
+                (direction_in, direction),
+                (colloid_in, colloid),
+                (count_in, count),
+                (speed_in, speed),
+                (slots_in, slots),
+                (flags_in, flags),
+                (shift_in, shift),
+                (phi_in, phi),
+                (solid_in, solid),
+            )
+        )
+    ]
+    for copy in small:
+        copy.start()
     for x in (0, 7, 1, 2, 3, 4, 5, 6):
         loads[x].start()
+    for copy in small:
+        copy.wait()
     for x in range(CX):
         order[pl.ds((x + 2) * PITCH + 8, CY), :] = phi[pl.ds(x * CY, CY), :]
     plane_low = flags[gx]
@@ -369,7 +399,7 @@
     build_rows(ext, phi, low_rows, DOWN_Y, 0, (0, 1))
     build_links(ext, site, direction, colloid, count, speed, slots, dmap, wmap, smap, part)
 
-    pl.semaphore_wait(barrier, FAR - 1 + 8 + NEAR - 1)
+    pl.semaphore_wait(barrier, FAR - 1 + 4 + NEAR - 1)
 
     def near_copy(k):
         t, device = near_id(k)
@@ -398,14 +428,14 @@
     for side, (src, dst, slab) in enumerate(
         ((up_face, below, slab_up), (down_face, above, slab_down))
     ):
-        for g in range(4):
+        for chip in range(2):
             faces.append(
                 pltpu.make_async_remote_copy(
                     src_ref=src,
                     dst_ref=dst.at[:, rows, :],
-                    send_sem=face_send.at[side, g],
+                    send_sem=face_send.at[side, chip],
                     recv_sem=face_recv.at[side, gy],
-                    device_id=(slab, g),
+                    device_id=(slab, 2 * chip + core),
                     device_id_type=MESH,
                 )
             )
@@ -448,6 +478,27 @@
     def _(k):
         far_copy(k).start()
 
+    def face_block(dst, g):
+        return dst.at[:, pl.ds(pl.multiple_of(g * CY, CY), CY), :]
+
+    relays = []
+    for chip in range(2):
+        for side, dst in enumerate((below, above)):
+            g = 2 * chip + core
+            block = face_block(dst, g)
+            pltpu.make_async_copy(block, block, face_recv.at[side, g]).wait()
+            relays.append(
+                pltpu.make_async_remote_copy(
+                    src_ref=block,
+                    dst_ref=block,
+                    send_sem=face_send.at[side, 2 + chip],
+                    recv_sem=face_recv.at[side, g],
+                    device_id=(gx, gy + 1 - 2 * core),
+                    device_id_type=MESH,
+                )
+            )
+            relays[-1].start()
+
     for copy in edges:
         copy.wait_recv()
     for f in range(5):
@@ -458,16 +509,17 @@
     order[pl.ds(2 * PITCH + 24, 8, stride=PITCH), :] = north[5]
     order[pl.ds(2 * PITCH + 25, 8, stride=PITCH), :] = north[6]
 
-    for side, dst in enumerate((below, above)):
-        for g in range(4):
-            block = dst.at[:, pl.ds(g * CY, CY), :]
+    for chip in range(2):
+        for side, dst in enumerate((below, above)):
+            g = 2 * chip + 1 - core
+            block = face_block(dst, g)
             pltpu.make_async_copy(block, block, face_recv.at[side, g]).wait()
 
     for f in range(7):
         for dst in (below, above):
             for r in range(0, 24, 8):
                 dst[f, pl.ds(64 + r, 8), :] = dst[f, pl.ds(r, 8), :]
-    s = shift[0]
+    s = shift[0, 0]
     begin_low = lax.rem(gy * CY - 2 - s * plane_low + 128, 64)
     begin_high = lax.rem(gy * CY - 2 + s * plane_high + 128, 64)
     for src, begin, components, layer, layers in (
@@ -482,37 +534,42 @@
                 order[pl.ds(l * PITCH + 6 + k, 8), :] = src[f, pl.ds(begin + k, 8), :]
 
     collide(ext, order, potential, solid, dmap, wmap, out, new_order)
-    stores = [
-        pltpu.make_async_copy(out.at[:, pl.ds(x * CY, CY), :], new_pop.at[:, pl.ds(x * CY, CY), :], out_sem.at[x])
-        for x in range(CX)
+    @pl.loop(1, FAR)
+    def _(k):
+        arrived(far, far_recv, lax.rem(z + k, FAR))
+
+    summed = total([far[h] for h in range(FAR)])
+    force[0:4, :] = pltpu.roll(summed, lax.rem(NZ - 4 * z, NZ), 1)
+
+    for copy in faces + edges + relays:
+        copy.wait_send()
+
+    @pl.loop(1, NEAR)
+    def _(k):
+        near_copy(k).wait_send()
+
+    @pl.loop(1, FAR)
+    def _(k):
+        far_copy(k).wait_send()
+
+
+def write(pop, order, force, new_pop, new_order, new_force, sem):
+    parts = [(0, 5), (5, 5), (10, 5), (15, 4)]
+    copies = [
+        pltpu.make_async_copy(pop.at[pl.ds(c, n)], new_pop.at[pl.ds(c, n)], sem.at[i])
+        for i, (c, n) in enumerate(parts)
     ]
-    for copy in stores:
+    copies.append(pltpu.make_async_copy(order, new_order, sem.at[4]))
+    for copy in copies:
         copy.start()
-
-    @pl.loop(1, FAR)
-    def _(k):
-        arrived(far, far_recv, lax.rem(z + k, FAR))
-
-    summed = total([far[h] for h in range(FAR)])
-    force[...] = pltpu.roll(summed, lax.rem(NZ - 4 * z, NZ), 1)[0:3, 0:4]
-
-    for copy in stores:
+    new_force[...] = force[0:3, 0:4]
+    for copy in copies:
         copy.wait()
-    for copy in faces + edges:
-        copy.wait_send()
-
-    @pl.loop(1, NEAR)
-    def _(k):
-        near_copy(k).wait_send()
-
-    @pl.loop(1, FAR)
-    def _(k):
-        far_copy(k).wait_send()
 
 
 VM = pl.BlockSpec(memory_space=pltpu.VMEM)
 SM = pl.BlockSpec(memory_space=pltpu.SMEM)
-HB = pl.BlockSpec(memory_space=pl.ANY)
+HB = pl.BlockSpec(memory_space=pltpu.HBM)
 
 
 def shaped(*dims, dtype=F32):
@@ -534,14 +591,27 @@
 ):
     new_pop, new_order, force = pl.pallas_call(
         step,
-        out_shape=(shaped(19, ROWS, NZ), shaped(ROWS, NZ), shaped(3, 4)),
-        in_specs=[HB, VM, VM, SM, SM, VM, VM, VM, SM, VM, VM],
-        out_specs=[HB, VM, VM],
+        out_shape=(
+            pltpu.VMEM((19, ROWS, NZ), F32),
+            pltpu.VMEM((ROWS, NZ), F32),
+            pltpu.VMEM((8, NZ), F32),
+        ),
+        in_specs=[HB] * 11,
+        out_specs=[VM] * 3,
         scratch_shapes=[
+            pltpu.VMEM((ROWS, NZ), F32),
+            pltpu.VMEM((ROWS, NZ), I32),
+            pltpu.SMEM((128,), I32),
+            pltpu.SMEM((1, 1), I32),
+            pltpu.VMEM((8, NZ), I32),
+            pltpu.VMEM((8, NZ), I32),
+            pltpu.VMEM((8, NZ), I32),
+            pltpu.SMEM((8,), I32),
+            pltpu.VMEM((3, 2048), F32),
+            pltpu.VMEM((16, NZ), I32),
             pltpu.VMEM((19, 10 * PITCH, NZ), F32),
             pltpu.VMEM((12 * PITCH, NZ), F32),
             pltpu.VMEM((10 * PITCH, NZ), F32),
-            pltpu.VMEM((19, ROWS, NZ), F32),
             pltpu.VMEM((7, 88, NZ), F32),
             pltpu.VMEM((7, 88, NZ), F32),
             pltpu.VMEM((7, 8, NZ), F32),
@@ -556,8 +626,7 @@
             pltpu.VMEM((ROWS, NZ), I32),
             pltpu.VMEM((ROWS, NZ), F32),
             pltpu.VMEM((ROWS, NZ), F32),
-            pltpu.SemaphoreType.DMA((CX,)),
-            pltpu.SemaphoreType.DMA((CX,)),
+            pltpu.SemaphoreType.DMA((CX + 10,)),
             pltpu.SemaphoreType.DMA((NEAR,)),
             pltpu.SemaphoreType.DMA((NEAR,)),
             pltpu.SemaphoreType.DMA((FAR,)),
@@ -574,7 +643,7 @@
         order_field.reshape(ROWS, NZ),
         solid_flags.reshape(ROWS, NZ),
         plane_flags,
-        shear_shift,
+        shear_shift.reshape(1, 1),
         link_site.reshape(8, NZ),
         link_dir.reshape(8, NZ),
         link_colloid.reshape(8, NZ),
@@ -582,6 +651,14 @@
         colloid_speed,
         colloid_slot.reshape(16, NZ),
     )
+    new_pop, new_order, force = pl.pallas_call(
+        write,
+        out_shape=(shaped(19, ROWS, NZ), shaped(ROWS, NZ), shaped(3, 4)),
+        in_specs=[VM] * 3,
+        out_specs=[HB, HB, VM],
+        scratch_shapes=[pltpu.SemaphoreType.DMA((5,))],
+        name="write",
+    )(*[pltpu.with_memory_space_constraint(v, pltpu.VMEM) for v in (new_pop, new_order, force)])
     return new_pop.reshape(populations.shape), new_order.reshape(order_field.shape), force
 
 

time: 39.6 us -> 33.5 us (0.85)
  local copies, waits for them, and re-layouts: 3.69 us -> 0 us
  Pallas kernels: 34.1 us -> 32 us
    unnamed x7 -> x0, local copies, waits for them, and re-layouts: 3.69 us -> none
    pallas_call x1 -> x2, Pallas kernels: 34.1 us -> 32 us  [the longest x1 30.4 us: per_device(): pl.pallas_call(step, out_shape=(pltpu.VMEM((19, ROWS, NZ), F32), pltpu.VM...]
where the time goes in v3:
time: 33.5 us; the launch traced here: 33.3 us
  Pallas kernels  32 us (96%)
  between operations  1.29 us (4%)
    pallas_call x1, Pallas kernels, per_device(): pl.pallas_call(step, out_shape=(pltpu.VMEM((19, ROWS, NZ), F32), pltpu.VM...  30.4 us
    pallas_call x1, Pallas kernels, per_device(): pl.pallas_call(write, out_shape=(shaped(19, ROWS, NZ), shaped(ROWS, NZ),...  1.66 us

profile of v3, /device:TPU:1, one launch (start us, length us, event | category | flops | bytes accessed | tf_op | source)
XLA Modules:
  0.0 33.3 jit_solution(4762592488352421813)
XLA Ops:
  1.3 30.4 %step.1 = (f32[19,128,128]{2,1,0:T(8,128)S(1)}, f32[128,128]{1,0:T(8,128)S(1)}, f32[8,128]{1,0:T(8,128)S(1)}) custom-call(f32[19,128,128]{2,1,0:T(8,128)} %bitcast.11, f32[128,128]{1,0:T(8,128)} %bitcast.12, s32[128,128]{1,0:T(8,128)} %bitcast.13, s32[128]{0:T(128)} %flags_in.1, s32[1,1]{1,0:T(1,128)} %bitcast.10.shift_in, s32[8,128]{1,0:T(8,128)} %bitcast.15, ...), custom_call_target="tpu_custom_call" | custom-call | tf_op jit(solution)/shard_map/step/pallas_call | solution.py:592
  31.7 1.7 %write.1 = (f32[19,128,128]{2,1,0:T(8,128)}, f32[128,128]{1,0:T(8,128)}, f32[3,4]{1,0:T(4,128)}) custom-call(f32[19,128,128]{2,1,0:T(8,128)S(1)} %get-tuple-element.9.pop, f32[128,128]{1,0:T(8,128)S(1)} %get-tuple-element.10.order, f32[8,128]{1,0:T(8,128)S(1)} %get-tuple-element.11.force), custom_call_target="tpu_custom_call" | custom-call | tf_op jit(solution)/shard_map/write/pallas_call | solution.py:654

commit v4 on v3

--- a/solution.py
+++ b/solution.py
@@ -323,16 +323,32 @@
     face_recv,
     row_send,
     row_recv,
+    told,
 ):
     gx, gy = lax.axis_index("gx"), lax.axis_index("gy")
     slab_up, slab_down = lax.rem(gx + 1, 128), lax.rem(gx + 127, 128)
     z, y, x_lo = lax.rem(gx // 4, 16), lax.rem(gx, 4), gx // 64
     near_me = x_lo * 16 + y * 4 + gy
     core = lax.rem(gy, 2)
-
-    def near_id(k):
-        t = lax.rem(near_me + k, NEAR)
-        return t, ((t // 16) * 64 + z * 4 + lax.rem(t // 4, 4), lax.rem(t, 4))
+    chip_x = gy // 2
+
+    peers = []
+    for flip_x in range(2):
+        for step_y in range(4):
+            for flip_chip in range(2):
+                for flip_core in range(2):
+                    hops = min(step_y, 4 - step_y) + (1 if flip_x else 2 * flip_chip)
+                    peers.append((-hops, flip_x, step_y, flip_chip, flip_core))
+    peers = [p[1:] for p in sorted(peers) if any(p[1:])]
+
+    def near_id(peer):
+        flip_x, step_y, flip_chip, flip_core = peer
+        to_x = 1 - x_lo if flip_x else x_lo
+        to_y = lax.rem(y + step_y, 4)
+        to_chip = 1 - chip_x if flip_chip else chip_x
+        to_core = 1 - core if flip_core else core
+        to_gy = 2 * to_chip + to_core
+        return to_x * 16 + to_y * 4 + to_gy, (to_x * 64 + z * 4 + to_y, to_gy)
 
     def far_id(k):
         h = lax.rem(z + k, FAR)
@@ -343,17 +359,18 @@
     def greet(device):
         pl.semaphore_signal(barrier, inc=1, device_id=device, device_id_type=MESH)
 
-    @pl.loop(1, FAR)
-    def _(k):
-        greet(far_id(k)[1])
+    def along(k):
+        return (x_lo * 64 + lax.rem(z + k + FAR, FAR) * 4 + y, gy)
+
+    for k in (4, -4, 3, -3, 2, -2, 1, -1):
+        greet(along(k))
 
     for slab in (slab_up, slab_down):
         for chip in range(2):
             greet((slab, 2 * chip + core))
 
-    @pl.loop(1, NEAR)
-    def _(k):
-        greet(near_id(k)[1])
+    for peer in peers:
+        greet(near_id(peer)[1])
 
     loads = [
         pltpu.make_async_copy(
@@ -399,7 +416,7 @@
     build_rows(ext, phi, low_rows, DOWN_Y, 0, (0, 1))
     build_links(ext, site, direction, colloid, count, speed, slots, dmap, wmap, smap, part)
 
-    pl.semaphore_wait(barrier, FAR - 1 + 4 + NEAR - 1)
+    pl.semaphore_wait(barrier, 8 + 4 + NEAR - 1)
 
     def near_copy(k):
         t, device = near_id(k)
@@ -454,9 +471,10 @@
             )
         )
 
-    @pl.loop(1, NEAR)
-    def _(k):
-        near_copy(k).start()
+    for device in (along(4), along(-4)):
+        pl.semaphore_signal(told, inc=1, device_id=device, device_id_type=MESH)
+    for peer in peers:
+        near_copy(peer).start()
 
     for copy in faces:
         copy.start()
@@ -468,14 +486,13 @@
     def arrived(buffer, sem, slot):
         pltpu.make_async_copy(buffer.at[slot], buffer.at[slot], sem.at[slot]).wait()
 
-    @pl.loop(1, NEAR)
-    def _(k):
-        arrived(near, near_recv, lax.rem(near_me + k, NEAR))
+    for peer in peers[::-1]:
+        arrived(near, near_recv, near_id(peer)[0])
 
     far[z] = total([near[t] for t in range(NEAR)])
 
-    @pl.loop(1, FAR)
-    def _(k):
+    pl.semaphore_wait(told, 2)
+    for k in (8, 7, 9, 6, 10, 5, 11, 4, 12, 3, 13, 2, 14, 1, 15):
         far_copy(k).start()
 
     def face_block(dst, g):
@@ -544,9 +561,8 @@
     for copy in faces + edges + relays:
         copy.wait_send()
 
-    @pl.loop(1, NEAR)
-    def _(k):
-        near_copy(k).wait_send()
+    for peer in peers:
+        near_copy(peer).wait_send()
 
     @pl.loop(1, FAR)
     def _(k):
@@ -635,6 +651,7 @@
             pltpu.SemaphoreType.DMA((2, 4)),
             pltpu.SemaphoreType.DMA((2,)),
             pltpu.SemaphoreType.DMA((2,)),
+            pltpu.SemaphoreType.REGULAR,
         ],
         compiler_params=pltpu.CompilerParams(collective_id=0, has_side_effects=True),
         name="step",

time: 33.5 us -> 31.6 us (0.943)
  Pallas kernels: 32 us -> 30.2 us
    pallas_call x1, Pallas kernels: 30.4 us -> 28.5 us  [per_device(): pl.pallas_call(step, out_shape=(pltpu.VMEM((19, ROWS, NZ), F32), pltpu.VM...]
where the time goes in v4:
time: 31.6 us; the launch traced here: 31.5 us
  Pallas kernels  30.2 us (96%)
  between operations  1.29 us (4%)
    pallas_call x1, Pallas kernels, per_device(): pl.pallas_call(step, out_shape=(pltpu.VMEM((19, ROWS, NZ), F32), pltpu.VM...  28.5 us
    pallas_call x1, Pallas kernels, per_device(): pl.pallas_call(write, out_shape=(shaped(19, ROWS, NZ), shaped(ROWS, NZ),...  1.66 us

profile of v4, /device:TPU:1, one launch (start us, length us, event | category | flops | bytes accessed | tf_op | source)
XLA Modules:
  0.0 31.5 jit_solution(18205797836738695113)
XLA Ops:
  1.3 28.5 %step.1 = (f32[19,128,128]{2,1,0:T(8,128)S(1)}, f32[128,128]{1,0:T(8,128)S(1)}, f32[8,128]{1,0:T(8,128)S(1)}) custom-call(f32[19,128,128]{2,1,0:T(8,128)} %bitcast.11, f32[128,128]{1,0:T(8,128)} %bitcast.12, s32[128,128]{1,0:T(8,128)} %bitcast.13, s32[128]{0:T(128)} %flags_in.1, s32[1,1]{1,0:T(1,128)} %bitcast.10.shift_in, s32[8,128]{1,0:T(8,128)} %bitcast.15, ...), custom_call_target="tpu_custom_call" | custom-call | tf_op jit(solution)/shard_map/step/pallas_call | solution.py:608
  29.8 1.7 %write.1 = (f32[19,128,128]{2,1,0:T(8,128)}, f32[128,128]{1,0:T(8,128)}, f32[3,4]{1,0:T(4,128)}) custom-call(f32[19,128,128]{2,1,0:T(8,128)S(1)} %get-tuple-element.9.pop, f32[128,128]{1,0:T(8,128)S(1)} %get-tuple-element.10.order, f32[8,128]{1,0:T(8,128)S(1)} %get-tuple-element.11.force), custom_call_target="tpu_custom_call" | custom-call | tf_op jit(solution)/shard_map/write/pallas_call | solution.py:671

commit v5 on v4

--- a/solution.py
+++ b/solution.py
@@ -159,34 +159,32 @@
             piece = left.astype(jnp.bfloat16).astype(F32)
             left = left - piece
             pieces[split].append(piece)
-    kind = sub & 3
+    even = (sub & 1) == 0
     left_rows, right_rows = [[], [], []], []
-    big = iota((NZ, NZ), 0)
-    for a in range(8):
-        spread = [
-            [jnp.broadcast_to(pieces[s][axis][a : a + 1], shape) for axis in range(3)]
-            for s in range(3)
-        ]
-        pattern = [
-            jnp.where(kind == 0, p[0], jnp.where(kind == 1, p[1], jnp.where(kind == 2, p[2], 0.0)))
-            for p in spread
-        ]
-        goes = jnp.broadcast_to(target[a : a + 1], (NZ, NZ)) == (big >> 2)
-        for s in range(3):
-            full = jnp.broadcast_to(pattern[s][None], (16, 8, NZ)).reshape(NZ, NZ)
-            left_rows[s].append(jnp.where(goes, full, 0.0).astype(jnp.bfloat16))
-        right_rows.append(
-            jnp.where(jnp.broadcast_to(column[a : a + 1], (NZ, NZ)) == big, 1.0, 0.0).astype(
-                jnp.bfloat16
-            )
-        )
+    row_of, column_of = iota((2 * NEAR, NZ), 0) >> 1, iota((NZ, NZ), 0)
+    for half in range(2):
+        for a in range(8):
+            spread = [
+                [jnp.broadcast_to(pieces[s][axis][a : a + 1], shape) for axis in range(3)]
+                for s in range(3)
+            ]
+            goes = jnp.broadcast_to(target[a : a + 1], (2 * NEAR, NZ)) == row_of
+            for s in range(3):
+                if half == 0:
+                    pattern = jnp.where(even, spread[s][0], spread[s][2])
+                else:
+                    pattern = jnp.where(even, spread[s][1], 0.0)
+                full = jnp.broadcast_to(pattern[None], (8, 8, NZ)).reshape(2 * NEAR, NZ)
+                left_rows[s].append(jnp.where(goes, full, 0.0).astype(jnp.bfloat16))
+            lands = jnp.broadcast_to(column[a : a + 1] + 64 * half, (NZ, NZ)) == column_of
+            right_rows.append(jnp.where(lands, 1.0, 0.0).astype(jnp.bfloat16))
     left_matrix = jnp.concatenate([jnp.concatenate(r, axis=1) for r in left_rows], axis=0)
     right_matrix = jnp.concatenate(right_rows, axis=1)
     product = lax.dot_general(
         left_matrix, right_matrix, (((1,), (1,)), ((), ())), preferred_element_type=F32
     )
-    product = product[0:NZ] + product[NZ : 2 * NZ] + product[2 * NZ :]
-    part[...] = product.reshape(NEAR, 4, NZ)
+    product = product[0:64] + product[64:128] + product[128:]
+    part[...] = product.reshape(NEAR, 2, NZ)
 
 
 def turn(value, step):
@@ -556,7 +554,10 @@
         arrived(far, far_recv, lax.rem(z + k, FAR))
 
     summed = total([far[h] for h in range(FAR)])
-    force[0:4, :] = pltpu.roll(summed, lax.rem(NZ - 4 * z, NZ), 1)
+    mine = pltpu.roll(summed, lax.rem(NZ - 4 * z, NZ), 1)
+    force[0:1, :] = mine[0:1, 0:4]
+    force[1:2, :] = pltpu.roll(mine, NZ // 2, 1)[0:1, 0:4]
+    force[2:3, :] = mine[1:2, 0:4]
 
     for copy in faces + edges + relays:
         copy.wait_send()
@@ -576,9 +577,9 @@
         for i, (c, n) in enumerate(parts)
     ]
     copies.append(pltpu.make_async_copy(order, new_order, sem.at[4]))
+    copies.append(pltpu.make_async_copy(force, new_force, sem.at[5]))
     for copy in copies:
         copy.start()
-    new_force[...] = force[0:3, 0:4]
     for copy in copies:
         copy.wait()
 
@@ -610,7 +611,7 @@
         out_shape=(
             pltpu.VMEM((19, ROWS, NZ), F32),
             pltpu.VMEM((ROWS, NZ), F32),
-            pltpu.VMEM((8, NZ), F32),
+            pltpu.VMEM((3, 4), F32),
         ),
         in_specs=[HB] * 11,
         out_specs=[VM] * 3,
@@ -636,9 +637,9 @@
             pltpu.VMEM((7, CY, NZ), F32),
             pltpu.VMEM((7, 8, NZ), F32),
             pltpu.VMEM((7, 8, NZ), F32),
-            pltpu.VMEM((NEAR, 4, NZ), F32),
-            pltpu.VMEM((NEAR, 4, NZ), F32),
-            pltpu.VMEM((FAR, 4, NZ), F32),
+            pltpu.VMEM((NEAR, 2, NZ), F32),
+            pltpu.VMEM((NEAR, 2, NZ), F32),
+            pltpu.VMEM((FAR, 2, NZ), F32),
             pltpu.VMEM((ROWS, NZ), I32),
             pltpu.VMEM((ROWS, NZ), F32),
             pltpu.VMEM((ROWS, NZ), F32),
@@ -672,8 +673,8 @@
         write,
         out_shape=(shaped(19, ROWS, NZ), shaped(ROWS, NZ), shaped(3, 4)),
         in_specs=[VM] * 3,
-        out_specs=[HB, HB, VM],
-        scratch_shapes=[pltpu.SemaphoreType.DMA((5,))],
+        out_specs=[HB, HB, HB],
+        scratch_shapes=[pltpu.SemaphoreType.DMA((6,))],
         name="write",
     )(*[pltpu.with_memory_space_constraint(v, pltpu.VMEM) for v in (new_pop, new_order, force)])
     return new_pop.reshape(populations.shape), new_order.reshape(order_field.shape), force

time: 31.6 us -> 30.4 us (0.962)
  Pallas kernels: 30.2 us -> 28.9 us
    pallas_call x1, Pallas kernels: 28.5 us -> 27.8 us  [per_device(): pl.pallas_call(step, out_shape=(pltpu.VMEM((19, ROWS, NZ), F32), pltpu.VM...]
    pallas_call x1, Pallas kernels: 1.66 us -> 1.1 us  [per_device(): pl.pallas_call(write, out_shape=(shaped(19, ROWS, NZ), shaped(ROWS, NZ),...]
where the time goes in v5:
time: 30.4 us; the launch traced here: 30.2 us
  Pallas kernels  28.9 us (95%)
  between operations  1.29 us (4%)
    pallas_call x1, Pallas kernels, per_device(): pl.pallas_call(step, out_shape=(pltpu.VMEM((19, ROWS, NZ), F32), pltpu.VM...  27.8 us
    pallas_call x1, Pallas kernels, per_device(): pl.pallas_call(write, out_shape=(shaped(19, ROWS, NZ), shaped(ROWS, NZ),...  1.1 us

profile of v5, /device:TPU:1, one launch (start us, length us, event | category | flops | bytes accessed | tf_op | source)
XLA Modules:
  0.0 30.2 jit_solution(13613793237475635528)
XLA Ops:
  1.3 27.8 %step.1 = (f32[19,128,128]{2,1,0:T(8,128)S(1)}, f32[128,128]{1,0:T(8,128)S(1)}, f32[3,4]{1,0:T(4,128)S(1)}) custom-call(f32[19,128,128]{2,1,0:T(8,128)} %bitcast.11, f32[128,128]{1,0:T(8,128)} %bitcast.12, s32[128,128]{1,0:T(8,128)} %bitcast.13, s32[128]{0:T(128)} %flags_in.1, s32[1,1]{1,0:T(1,128)} %bitcast.10.shift_in, s32[8,128]{1,0:T(8,128)} %bitcast.15, ...), custom_call_target="tpu_custom_call" | custom-call | tf_op jit(solution)/shard_map/step/pallas_call | solution.py:609
  29.1 1.1 %write.1 = (f32[19,128,128]{2,1,0:T(8,128)}, f32[128,128]{1,0:T(8,128)}, f32[3,4]{1,0:T(4,128)}) custom-call(f32[19,128,128]{2,1,0:T(8,128)S(1)} %get-tuple-element.9.pop, f32[128,128]{1,0:T(8,128)S(1)} %get-tuple-element.10.order, f32[3,4]{1,0:T(4,128)S(1)} %get-tuple-element.11.force), custom_call_target="tpu_custom_call" | custom-call | tf_op jit(solution)/shard_map/write/pallas_call | solution.py:672
